TPU v7x, 32 devices: a whole 2x2x4 slice. The times are simulated.
32 devices in a mesh: grp: 2 (over y), date: 4 (over x, core), strip: 4 (over z).
Axes of the slice: x: 2, y: 2, z: 4, core: 2. Of those that a mesh axis runs over, the one named last changes fastest.
Arguments:
- acquisitions: bfloat16 [16, 64, 2, 16384], P(('grp', 'date'), 'strip'), parts along dimension 0, may hold values from -22 to 22
- partners: int32 [2, 16], P(None, ('grp', 'date')), parts along dimension 1, may hold values from 0 to 7, as said below
- band_shifts: int32 [2, 16], P(None, ('grp', 'date')), parts along dimension 1, may hold values from -24 to 24
Outputs:
- interferograms: bfloat16 [2, 16, 2, 64, 4096], P(None, ('grp', 'date'), None, 'strip'), parts along dimension 1
- coherence: bfloat16 [2, 16, 64, 4096], P(None, ('grp', 'date'), 'strip'), parts along dimension 1
There are 2 independent parts, one for each index of `grp`. A program takes and returns all parts, laid end to end along the dimension named above; each array names one. Nothing has to cross between parts.
Inputs may be any that keep to these rules, and one draw needn't show every extreme that they name: For each matching m and each date group g (dates g * 2 to (g + 1) * 2 - 1), the partners of the group's dates are the 2 different dates of one other group: g with its lowest bit flipped for m = 0, and (g + 2) modulo 4 for m = 1.
All inputs are finite; a program needn't handle non-finite values.
Results may differ from a plain program's by a relative error of at most 0.0075.
Values may be sent and summed in bfloat16 or wider, within the bound.
A program may use at most 64 MiB of HBM per device.

v0:
```python
import math

import jax
import jax.numpy as jnp
from jax import lax
from jax.experimental import pallas as pl
from jax.experimental.pallas import tpu as pltpu
from jax.sharding import PartitionSpec as P

band_width = 0.8
bin_count = 256.0
epsilon = 1e-06
below = 10
above = 9
lanes = 128
segments = 16


def partner(block, axis, distance):
    count = lax.axis_size(axis)
    route = []
    for low in range(count):
        high = low | 1 << distance
        if high != low and high < count:
            route += [(low, high), (high, low)]
    return lax.ppermute(block, axis, route)


def make_taps(shift_bins):
    positions = jnp.arange(64, dtype=jnp.float32)
    centred = positions - 31.5
    hamming = 0.54 - 0.46 * jnp.cos(2.0 * math.pi * positions / 63.0)
    lowpass = hamming * band_width * jnp.sinc(band_width * centred)
    angles = 2.0 * math.pi * shift_bins.astype(jnp.float32)[..., None] * centred / bin_count
    taps = jnp.stack([lowpass * jnp.cos(angles), lowpass * jnp.sin(angles)], axis=-2)
    taps = taps.astype(jnp.bfloat16).astype(jnp.float32)
    zeros = jnp.zeros(taps.shape[:-1] + (64,), jnp.float32)
    return jnp.concatenate([taps[..., 32:], zeros, taps[..., :32]], axis=-1)


def circulant(row):
    block = jnp.broadcast_to(row, (32, lanes))
    parts = [pltpu.roll(block, phase, 1, stride=4, stride_axis=0) for phase in range(4)]
    return jnp.concatenate(parts, axis=0).T


def build_weights(taps_ref, weight_ref):
    real_part = circulant(taps_ref[0, 0:1, :])
    imag_part = circulant(taps_ref[0, 1:2, :])
    k = lax.broadcasted_iota(jnp.int32, (lanes, lanes), 0)
    c = lax.broadcasted_iota(jnp.int32, (lanes, lanes), 1)
    t = 4 * (c & 31) + (c >> 5)
    inside = jnp.abs(k - t) < 64
    for place, mask in ((0, inside), (1, jnp.logical_not(inside))):
        re = jnp.where(mask, real_part, 0.0)
        im = jnp.where(mask, imag_part, 0.0)
        weight_ref[place, 0:lanes, 0:lanes] = re.astype(jnp.bfloat16)
        weight_ref[place, 0:lanes, lanes:] = im.astype(jnp.bfloat16)
        weight_ref[place, lanes:, 0:lanes] = (-im).astype(jnp.bfloat16)
        weight_ref[place, lanes:, lanes:] = re.astype(jnp.bfloat16)


def looks_kernel(
    row_step, slots_ref, taps_ref, first_ref, second_ref, looks_ref, low_ref, high_ref, weight_ref, band_ref
):
    rows, tiles = first_ref.shape[1], first_ref.shape[2]
    build_weights(taps_ref, weight_ref)
    lane = lax.broadcasted_iota(jnp.int32, (segments, 2 * lanes), 1) & (lanes - 1)
    segment = lax.broadcasted_iota(jnp.int32, (segments, 2 * lanes), 0)
    from_before = jnp.where(lane >= 64, 1.0, 0.0).astype(jnp.bfloat16)
    from_after = jnp.where(lane < 64, 1.0, 0.0).astype(jnp.bfloat16)

    def filter_rows(source_ref, start, slot):
        current, edges = [], []
        for i in range(row_step):
            x = [source_ref[0, start + i, q] for q in range(tiles)]
            head = pltpu.roll(x[-1].astype(jnp.float32), 1, 0)
            head = jnp.where(segment == 0, 0.0, head).astype(jnp.bfloat16)
            tail = pltpu.roll(x[0].astype(jnp.float32), segments - 1, 0)
            tail = jnp.where(segment == segments - 1, 0.0, tail).astype(jnp.bfloat16)
            y = [head] + x + [tail]
            current += x
            edges += [y[q] * from_before + y[q + 2] * from_after for q in range(tiles)]
        current = jnp.concatenate(current, axis=0)
        edges = jnp.concatenate(edges, axis=0)
        out = jnp.dot(current, weight_ref[0], preferred_element_type=jnp.float32)
        out = out + jnp.dot(edges, weight_ref[1], preferred_element_type=jnp.float32)
        band_ref[slot] = out.astype(jnp.bfloat16).reshape(row_step, tiles, segments, 2 * lanes)

    group = lax.broadcasted_iota(jnp.int32, (segments, lanes), 1) >> 5
    outer = (group == 0) | (group == 3)
    lower = group < 2
    even = (group & 1) == 0

    def pool(v):
        a = jnp.where(outer, v[0], v[2]) + pltpu.roll(jnp.where(outer, v[2], v[0]), 64, 1)
        b = jnp.where(lower, v[1], v[3]) + pltpu.roll(jnp.where(lower, v[3], v[1]), 64, 1)
        return jnp.where(even, a, b) + pltpu.roll(jnp.where(even, b, a), 32, 1)

    def step(index, carry):
        start = index * row_step
        filter_rows(first_ref, start, 0)
        filter_rows(second_ref, start, 1)
        for i in range(row_step):
            for a in range(tiles // 4):
                planes = [[], [], [], []]
                for b in range(4):
                    q = 4 * a + b
                    one = band_ref[0, i, q].astype(jnp.float32)
                    two = band_ref[1, i, q].astype(jnp.float32)
                    fr, fi = one[:, :lanes], one[:, lanes:]
                    sr, si = two[:, :lanes], two[:, lanes:]
                    planes[0].append(fr * sr + fi * si)
                    planes[1].append(fi * sr - fr * si)
                    planes[2].append(fr * fr + fi * fi)
                    planes[3].append(sr * sr + si * si)
                for p in range(4):
                    looks_ref[0, start + i, p, a] = pool(planes[p])
        return carry

    lax.fori_loop(0, rows // row_step, step, 0)
    low_ref[...] = looks_ref[:, rows - below :].astype(jnp.bfloat16)
    high_ref[...] = looks_ref[:, :above].astype(jnp.bfloat16)


def pair_looks(slots, taps, own, other):
    dates, rows, tiles = own.shape[:3]
    row_step = 4
    tail = (4, tiles // 4, segments, lanes)
    image = (1, rows, tiles, segments, 2 * lanes)
    return pl.pallas_call(
        lambda *refs: looks_kernel(row_step, *refs),
        out_shape=(
            jax.ShapeDtypeStruct((dates, rows) + tail, jnp.float32),
            jax.ShapeDtypeStruct((dates, below) + tail, jnp.bfloat16),
            jax.ShapeDtypeStruct((dates, above) + tail, jnp.bfloat16),
        ),
        grid_spec=pltpu.PrefetchScalarGridSpec(
            num_scalar_prefetch=1,
            grid=(dates,),
            in_specs=[
                pl.BlockSpec((1, 2, lanes), lambda i, s: (i, 0, 0)),
                pl.BlockSpec(image, lambda i, s: (i, 0, 0, 0, 0)),
                pl.BlockSpec(image, lambda i, s: (s[i], 0, 0, 0, 0)),
            ],
            out_specs=[
                pl.BlockSpec((1, n) + tail, lambda i, s: (i, 0, 0, 0, 0, 0)) for n in (rows, below, above)
            ],
            scratch_shapes=[
                pltpu.VMEM((2, 2 * lanes, 2 * lanes), jnp.bfloat16),
                pltpu.VMEM((2, row_step, tiles, segments, 2 * lanes), jnp.bfloat16),
            ],
        ),
        compiler_params=pltpu.CompilerParams(vmem_limit_bytes=40 << 20),
        cost_estimate=pl.CostEstimate(
            flops=dates * rows * tiles * segments * 2 * 2 * 512 * 256,
            bytes_accessed=dates * rows * tiles * segments * 256 * 8,
            transcendentals=0,
        ),
        name="looks",
    )(slots, taps, own, other)


def finish_kernel(looks_ref, low_ref, high_ref, *rest):
    cross_ref, coherence_ref, turn_ref = rest[-3:]
    rows, halves = looks_ref.shape[1], looks_ref.shape[3]
    for a in range(halves):
        for h in range(0, segments, 8):
            window = []
            for p in range(4):
                e = [low_ref[0, i, p, a].astype(jnp.float32)[h : h + 8] for i in range(below)]
                e += [looks_ref[0, i, p, a, h : h + 8, :] for i in range(rows)]
                e += [high_ref[0, i, p, a].astype(jnp.float32)[h : h + 8] for i in range(above)]
                s2 = [e[i] + e[i + 1] for i in range(len(e) - 1)]
                s4 = [s2[i] + s2[i + 2] for i in range(len(s2) - 2)]
                s8 = [s4[i] + s4[i + 4] for i in range(len(s4) - 4)]
                window.append([s8[r] + s8[r + 8] + s4[r + 16] for r in range(rows)])
            for r in range(rows):
                cr, ci, pf, ps = (window[p][r] for p in range(4))
                spot = pl.ds(h * rows + r, 8, stride=rows)
                turn_ref[0, spot, :] = cr / 80.0
                turn_ref[1, spot, :] = ci / 80.0
                turn_ref[2, spot, :] = jnp.sqrt(cr * cr + ci * ci) * lax.rsqrt(pf * ps + epsilon)
        for s in range(segments):
            column = (s * halves + a) * lanes
            for k in range(2):
                cross_ref[0, 0, k, :, column : column + lanes] = turn_ref[
                    k, s * rows : (s + 1) * rows, :
                ].astype(jnp.bfloat16)
            coherence_ref[0, 0, :, column : column + lanes] = turn_ref[
                2, s * rows : (s + 1) * rows, :
            ].astype(jnp.bfloat16)


def finish(match, looks, low, high, so_far):
    dates, rows = looks.shape[:2]
    tail = looks.shape[2:]
    columns = tail[1] * segments * lanes
    block = lambda n: pl.BlockSpec((1, n) + tail, lambda i: (i, 0, 0, 0, 0, 0))
    anywhere = pl.BlockSpec(memory_space=pl.ANY)
    return pl.pallas_call(
        finish_kernel,
        out_shape=(
            jax.ShapeDtypeStruct((2, dates, 2, rows, columns), jnp.bfloat16),
            jax.ShapeDtypeStruct((2, dates, rows, columns), jnp.bfloat16),
        ),
        grid=(dates,),
        in_specs=[block(rows), block(below), block(above)] + [anywhere] * len(so_far),
        out_specs=[
            pl.BlockSpec((1, 1, 2, rows, columns), lambda i: (match, i, 0, 0, 0)),
            pl.BlockSpec((1, 1, rows, columns), lambda i: (match, i, 0, 0)),
        ],
        scratch_shapes=[pltpu.VMEM((3, segments * rows, lanes), jnp.float32)],
        input_output_aliases={3 + i: i for i in range(len(so_far))},
        compiler_params=pltpu.CompilerParams(vmem_limit_bytes=40 << 20),
        cost_estimate=pl.CostEstimate(
            flops=dates * rows * columns * 40, bytes_accessed=dates * rows * columns * 32, transcendentals=0
        ),
        name="finish",
    )(looks, low, high, *so_far)


def per_device(acquisitions, partners, band_shifts):
    dates, rows, _, samples = acquisitions.shape
    tiles = samples // (segments * lanes)
    top_bit = lax.axis_size("date").bit_length() - 2
    strips = lax.axis_size("strip")
    upward = [(i, i + 1) for i in range(strips - 1)]
    downward = [(i + 1, i) for i in range(strips - 1)]
    taps = make_taps(band_shifts)
    slots = partners % dates
    own = acquisitions.reshape(dates, rows, 2, segments, tiles, lanes)
    own = own.transpose(0, 1, 4, 3, 2, 5).reshape(dates, rows, tiles, segments, 2 * lanes)
    far = partner(own, "date", top_bit)
    near = partner(own, "date", 0)
    results = ()
    for match, other in ((0, near), (1, far)):
        looks, low, high = pair_looks(slots[match], taps[match], own, other)
        low = lax.ppermute(low, "strip", upward)
        high = lax.ppermute(high, "strip", downward)
        results = finish(match, looks, low, high, results)
    return tuple(results)


def solution(mesh):
    in_specs = (
        P(("grp", "date"), "strip", None, None),
        P(None, ("grp", "date")),
        P(None, ("grp", "date")),
    )
    out_specs = (
        P(None, ("grp", "date"), None, "strip", None),
        P(None, ("grp", "date"), "strip", None),
    )
    return jax.shard_map(
        per_device, mesh=mesh, in_specs=in_specs, out_specs=out_specs, check_vma=False
    )
```

profile of v0, /device:TPU:0, one launch (start us, length us, event | category | flops | bytes accessed | tf_op | source)
XLA Modules:
  0.0 101.8 jit_solution(12330634154378247538)
XLA Ops:
  0.6 3.3 %reshape.77 = bf16[2,16,2,16,8,128]{5,4,3,2,1,0:T(8,128)(2,1)S(1)} reshape(bf16[2,16,2,16384]{3,2,1,0:T(2,128)(2,1)} %param.3) | data formatting | bytes 4194304 | tf_op jit(solution)/shard_map/reshape | solution.py:232
  4.0 3.5 %copy.12 = bf16[2,16,2,16,8,128]{5,2,3,4,1,0:T(2,128)(2,1)} copy(bf16[2,16,2,16,8,128]{5,4,3,2,1,0:T(8,128)(2,1)S(1)} %reshape.77) | data formatting | bytes 4194304 | tf_op jit(solution)/shard_map/reshape | solution.py:232
  7.5 0.0 copy-start
  7.5 0.0 copy-start.1
  7.5 3.2 %reshape.78.refs_2_ = bf16[2,16,8,16,256]{4,3,2,1,0:T(8,128)(2,1)S(1)} reshape(bf16[2,16,8,16,2,128]{5,4,3,2,1,0:T(2,128)(2,1)} %bitcast.12) | data formatting | bytes 4194304 | tf_op jit(solution)/shard_map/reshape | solution.py:233
  10.7 0.5 collective-permute-start.3
  11.2 2.6 %collective-permute-start = (bf16[2,16,8,16,256]{4,3,2,1,0:T(8,128)(2,1)S(1)}, bf16[2,16,8,16,256]{4,3,2,1,0:T(8,128)(2,1)S(1)}, u32[]{:S(2)}, u32[]{:S(2)}) collective-permute-start(bf16[2,16,8,16,256]{4,3,2,1,0:T(8,128)(2,1)S(1)} %reshape.78.refs_2_), channel_id=1, source_target_pairs={{0,8},{8,0},{4,12},{12,4},{1,9},{9,1},{5,13},{13,5},{2,10},{10,2},... | collective-permute-start | bytes 6291464 | tf_op jit(solution)/shard_map/ppermute | solution.py:26
  13.8 0.1 pad.1.clone
  13.8 0.1 fusion.5
  13.9 0.0 copy-done
  13.9 0.1 multiply_convert_fusion.1
  14.1 0.0 copy-done.1
  14.1 0.1 fusion.10
  14.2 0.1 pad_maximum_fusion
  14.3 0.7 collective-permute-done.3.refs_3_
  15.0 6.7 %looks.3 = (f32[2,16,4,2,16,128]{5,4,3,2,1,0:T(8,128)S(1)}, bf16[2,10,4,2,16,128]{5,4,3,2,1,0:T(8,128)(2,1)S(1)}, bf16[2,9,4,2,16,128]{5,4,3,2,1,0:T(8,128)(2,1)S(1)}) custom-call(s32[2]{0:T(128)S(1)} %get-tuple-element.24.refs_0_, f32[2,2,128]{2,1,0:T(2,128)S(1)} %get-tuple-element.18.refs_1_, bf16[2,16,8,16,256]{4,3,2,1,0:T(8,128)(2,1)S(1)} %reshape.78.refs_2_, ...), custom_call_target="tpu_custom_call" | custom-call | flops 2147483648 | bytes 8388608 | tf_op jit(solution)/shard_map/looks/pallas_call | solution.py:131
  21.7 4.9 %collective-permute-start.4 = (bf16[2,10,4,2,16,128]{5,4,3,2,1,0:T(8,128)(2,1)S(1)}, bf16[2,10,4,2,16,128]{5,4,3,2,1,0:T(8,128)(2,1)S(1)}, u32[]{:S(2)}, u32[]{:S(2)}) collective-permute-start(bf16[2,10,4,2,16,128]{5,4,3,2,1,0:T(8,128)(2,1)S(1)} %get-tuple-element.14), channel_id=1, source_target_pairs={{0,1},{1,2},{2,3},{4,5},{5,6},{6,7},{8,9},{9,10},{10,11},{12,13},{... | collective-permute-start | bytes 1966088 | tf_op jit(solution)/shard_map/ppermute | solution.py:239
  26.6 33.4 %collective-permute-done.refs_3_ = bf16[2,16,8,16,256]{4,3,2,1,0:T(8,128)(2,1)S(1)} collective-permute-done((bf16[2,16,8,16,256]{4,3,2,1,0:T(8,128)(2,1)S(1)}, bf16[2,16,8,16,256]{4,3,2,1,0:T(8,128)(2,1)S(1)}, u32[]{:S(2)}, u32[]{:S(2)}) %collective-permute-start) | collective-permute-done | bytes 2097184 | tf_op jit(solution)/shard_map/ppermute | solution.py:26
  60.0 6.7 %looks.2 = (f32[2,16,4,2,16,128]{5,4,3,2,1,0:T(8,128)S(1)}, bf16[2,10,4,2,16,128]{5,4,3,2,1,0:T(8,128)(2,1)S(1)}, bf16[2,9,4,2,16,128]{5,4,3,2,1,0:T(8,128)(2,1)S(1)}) custom-call(s32[2]{0:T(128)S(1)} %get-tuple-element.25.refs_0_, f32[2,2,128]{2,1,0:T(2,128)S(1)} %get-tuple-element.19.refs_1_, bf16[2,16,8,16,256]{4,3,2,1,0:T(8,128)(2,1)S(1)} %reshape.78.refs_2_, ...), custom_call_target="tpu_custom_call" | custom-call | flops 2147483648 | bytes 8388608 | tf_op jit(solution)/shard_map/looks/pallas_call | solution.py:131
  66.7 3.8 %collective-permute-start.1 = (bf16[2,10,4,2,16,128]{5,4,3,2,1,0:T(8,128)(2,1)S(1)}, bf16[2,10,4,2,16,128]{5,4,3,2,1,0:T(8,128)(2,1)S(1)}, u32[]{:S(2)}, u32[]{:S(2)}) collective-permute-start(bf16[2,10,4,2,16,128]{5,4,3,2,1,0:T(8,128)(2,1)S(1)} %get-tuple-element.11), channel_id=1, source_target_pairs={{0,1},{1,2},{2,3},{4,5},{5,6},{6,7},{8,9},{9,10},{10,11},{12,13},{... | collective-permute-start | bytes 1966088 | tf_op jit(solution)/shard_map/ppermute | solution.py:239
  70.5 1.3 %collective-permute-start.5 = (bf16[2,9,4,2,16,128]{5,4,3,2,1,0:T(8,128)(2,1)S(1)}, bf16[2,9,4,2,16,128]{5,4,3,2,1,0:T(8,128)(2,1)S(1)}, u32[]{:S(2)}, u32[]{:S(2)}) collective-permute-start(bf16[2,9,4,2,16,128]{5,4,3,2,1,0:T(8,128)(2,1)S(1)} %get-tuple-element.15), channel_id=1, source_target_pairs={{1,0},{2,1},{3,2},{5,4},{6,5},{7,6},{9,8},{10,9},{11,10},{13,12},{... | collective-permute-start | bytes 1769480 | tf_op jit(solution)/shard_map/ppermute | solution.py:240
  71.8 1.3 %collective-permute-start.2 = (bf16[2,9,4,2,16,128]{5,4,3,2,1,0:T(8,128)(2,1)S(1)}, bf16[2,9,4,2,16,128]{5,4,3,2,1,0:T(8,128)(2,1)S(1)}, u32[]{:S(2)}, u32[]{:S(2)}) collective-permute-start(bf16[2,9,4,2,16,128]{5,4,3,2,1,0:T(8,128)(2,1)S(1)} %get-tuple-element.12), channel_id=1, source_target_pairs={{1,0},{2,1},{3,2},{5,4},{6,5},{7,6},{9,8},{10,9},{11,10},{13,12},{... | collective-permute-start | bytes 1769480 | tf_op jit(solution)/shard_map/ppermute | solution.py:240
  73.1 15.6 %collective-permute-done.5.high_ref = bf16[2,9,4,2,16,128]{5,4,3,2,1,0:T(8,128)(2,1)S(1)} collective-permute-done((bf16[2,9,4,2,16,128]{5,4,3,2,1,0:T(8,128)(2,1)S(1)}, bf16[2,9,4,2,16,128]{5,4,3,2,1,0:T(8,128)(2,1)S(1)}, u32[]{:S(2)}, u32[]{:S(2)}) %collective-permute-start.5) | collective-permute-done | bytes 589856 | tf_op jit(solution)/shard_map/ppermute | solution.py:240
  88.7 0.0 collective-permute-done.4.low_ref
  88.7 2.1 %finish.2 = (bf16[2,2,2,16,4096]{4,3,2,1,0:T(8,128)(2,1)}, bf16[2,2,16,4096]{3,2,1,0:T(8,128)(2,1)}) custom-call(f32[2,16,4,2,16,128]{5,4,3,2,1,0:T(8,128)S(1)} %get-tuple-element.13.looks_ref, bf16[2,10,4,2,16,128]{5,4,3,2,1,0:T(8,128)(2,1)S(1)} %collective-permute-done.4.low_ref, bf16[2,9,4,2,16,128]{5,4,3,2,1,0:T(8,128)(2,1)S(1)} %collective-permute-done.5.high_ref), custom_call_target="tpu_custom_call" | custom-call | flops 5242880 | bytes 4194304 | tf_op jit(solution)/shard_map/finish/pallas_call | solution.py:201
  90.8 8.9 %collective-permute-done.2.high_ref = bf16[2,9,4,2,16,128]{5,4,3,2,1,0:T(8,128)(2,1)S(1)} collective-permute-done((bf16[2,9,4,2,16,128]{5,4,3,2,1,0:T(8,128)(2,1)S(1)}, bf16[2,9,4,2,16,128]{5,4,3,2,1,0:T(8,128)(2,1)S(1)}, u32[]{:S(2)}, u32[]{:S(2)}) %collective-permute-start.2) | collective-permute-done | bytes 589856 | tf_op jit(solution)/shard_map/ppermute | solution.py:240
  99.7 0.0 collective-permute-done.1.low_ref
  99.7 2.1 %finish.3 = (bf16[2,2,2,16,4096]{4,3,2,1,0:T(8,128)(2,1)}, bf16[2,2,16,4096]{3,2,1,0:T(8,128)(2,1)}) custom-call(f32[2,16,4,2,16,128]{5,4,3,2,1,0:T(8,128)S(1)} %get-tuple-element.10.looks_ref, bf16[2,10,4,2,16,128]{5,4,3,2,1,0:T(8,128)(2,1)S(1)} %collective-permute-done.1.low_ref, ...), custom_call_target="tpu_custom_call", output_to_operand_aliasing={{0}: (3, {}), {1}: (4, {})} | custom-call | flops 5242880 | bytes 4194304 | tf_op jit(solution)/shard_map/finish/pallas_call | solution.py:201
  (8 shorter events, 0.0 us)
Async XLA Ops:
  7.5 6.4 %copy-start = (s32[2,2]{1,0:T(2,128)S(1)}, s32[2,2]{1,0:T(2,128)}, u32[]{:S(2)}) copy-start(s32[2,2]{1,0:T(2,128)} %param.5) | copy-start | bytes 52
  7.5 6.6 %copy-start.1 = (s32[2,2]{1,0:T(2,128)S(1)}, s32[2,2]{1,0:T(2,128)}, u32[]{:S(2)}) copy-start(s32[2,2]{1,0:T(2,128)} %param.4) | copy-start | bytes 52
  10.7 4.3 %collective-permute-start.3 = (bf16[2,16,8,16,256]{4,3,2,1,0:T(8,128)(2,1)S(1)}, bf16[2,16,8,16,256]{4,3,2,1,0:T(8,128)(2,1)S(1)}, u32[]{:S(2)}, u32[]{:S(2)}) collective-permute-start(bf16[2,16,8,16,256]{4,3,2,1,0:T(8,128)(2,1)S(1)} %reshape.78.refs_2_), channel_id=1, source_target_pairs={{0,4},{4,0},{8,12},{12,8},{1,5},{5,1},{9,13},{13,9},{2,6},{6,2},{1... | collective-permute-start | bytes 6291464 | tf_op jit(solution)/shard_map/ppermute | solution.py:26
  11.2 48.8 %collective-permute-start = (bf16[2,16,8,16,256]{4,3,2,1,0:T(8,128)(2,1)S(1)}, bf16[2,16,8,16,256]{4,3,2,1,0:T(8,128)(2,1)S(1)}, u32[]{:S(2)}, u32[]{:S(2)}) collective-permute-start(bf16[2,16,8,16,256]{4,3,2,1,0:T(8,128)(2,1)S(1)} %reshape.78.refs_2_), channel_id=1, source_target_pairs={{0,8},{8,0},{4,12},{12,4},{1,9},{9,1},{5,13},{13,5},{2,10},{10,2},... | collective-permute-start | bytes 6291464 | tf_op jit(solution)/shard_map/ppermute | solution.py:26
  21.7 67.0 %collective-permute-start.4 = (bf16[2,10,4,2,16,128]{5,4,3,2,1,0:T(8,128)(2,1)S(1)}, bf16[2,10,4,2,16,128]{5,4,3,2,1,0:T(8,128)(2,1)S(1)}, u32[]{:S(2)}, u32[]{:S(2)}) collective-permute-start(bf16[2,10,4,2,16,128]{5,4,3,2,1,0:T(8,128)(2,1)S(1)} %get-tuple-element.14), channel_id=1, source_target_pairs={{0,1},{1,2},{2,3},{4,5},{5,6},{6,7},{8,9},{9,10},{10,11},{12,13},{... | collective-permute-start | bytes 1966088 | tf_op jit(solution)/shard_map/ppermute | solution.py:239
  66.7 32.9 %collective-permute-start.1 = (bf16[2,10,4,2,16,128]{5,4,3,2,1,0:T(8,128)(2,1)S(1)}, bf16[2,10,4,2,16,128]{5,4,3,2,1,0:T(8,128)(2,1)S(1)}, u32[]{:S(2)}, u32[]{:S(2)}) collective-permute-start(bf16[2,10,4,2,16,128]{5,4,3,2,1,0:T(8,128)(2,1)S(1)} %get-tuple-element.11), channel_id=1, source_target_pairs={{0,1},{1,2},{2,3},{4,5},{5,6},{6,7},{8,9},{9,10},{10,11},{12,13},{... | collective-permute-start | bytes 1966088 | tf_op jit(solution)/shard_map/ppermute | solution.py:239
  70.5 18.2 %collective-permute-start.5 = (bf16[2,9,4,2,16,128]{5,4,3,2,1,0:T(8,128)(2,1)S(1)}, bf16[2,9,4,2,16,128]{5,4,3,2,1,0:T(8,128)(2,1)S(1)}, u32[]{:S(2)}, u32[]{:S(2)}) collective-permute-start(bf16[2,9,4,2,16,128]{5,4,3,2,1,0:T(8,128)(2,1)S(1)} %get-tuple-element.15), channel_id=1, source_target_pairs={{1,0},{2,1},{3,2},{5,4},{6,5},{7,6},{9,8},{10,9},{11,10},{13,12},{... | collective-permute-start | bytes 1769480 | tf_op jit(solution)/shard_map/ppermute | solution.py:240
  71.8 27.8 %collective-permute-start.2 = (bf16[2,9,4,2,16,128]{5,4,3,2,1,0:T(8,128)(2,1)S(1)}, bf16[2,9,4,2,16,128]{5,4,3,2,1,0:T(8,128)(2,1)S(1)}, u32[]{:S(2)}, u32[]{:S(2)}) collective-permute-start(bf16[2,9,4,2,16,128]{5,4,3,2,1,0:T(8,128)(2,1)S(1)} %get-tuple-element.12), channel_id=1, source_target_pairs={{1,0},{2,1},{3,2},{5,4},{6,5},{7,6},{9,8},{10,9},{11,10},{13,12},{... | collective-permute-start | bytes 1769480 | tf_op jit(solution)/shard_map/ppermute | solution.py:240
where the time goes:
time: 102 us
  waiting for transfers between devices  58.5 us (57%)
  Pallas kernels  17.6 us (17%)
  starting transfers between devices  14.3 us (14%)
  local copies, waits for them, and re-layouts  10.2 us (10%)
    ppermute x2, waiting for transfers between devices, partner(): return lax.ppermute(block, axis, route)  34 us
    ppermute x2, waiting for transfers between devices, per_device(): high = lax.ppermute(high, 'strip', downward)  24.5 us
    pallas_call x2, Pallas kernels, pair_looks(): pl.pallas_call(lambda *refs: looks_kernel(row_step, *refs), out_shape=(ja...  13.5 us
    ppermute x2, starting transfers between devices, per_device(): low = lax.ppermute(low, 'strip', upward)  8.68 us
    reshape x2, local copies, waits for them, and re-layouts, per_device(): own = acquisitions.reshape(dates, rows, 2, segments, tiles, lanes)  6.85 us
    pallas_call x2, Pallas kernels, finish(): pl.pallas_call(finish_kernel, out_shape=(jax.ShapeDtypeStruct((2, dates,...  4.16 us
    reshape x1, local copies, waits for them, and re-layouts, per_device(): own.transpose(0, 1, 4, 3, 2, 5)  3.18 us
    ppermute x2, starting transfers between devices, partner(): return lax.ppermute(block, axis, route)  3.08 us
  transfers between devices with their start and end apart: 6, of which 4 were waited for; matrix products, arithmetic and copies ran while one was open for 0% of the time, Pallas kernels for 15%

commit v1 on v0

--- a/solution.py
+++ b/solution.py
@@ -4,6 +4,8 @@
 import jax.numpy as jnp
 from jax import lax
 from jax.experimental import pallas as pl
+from jax.experimental.layout import Layout, with_layout_constraint
+
 from jax.experimental.pallas import tpu as pltpu
 from jax.sharding import PartitionSpec as P
 
@@ -61,7 +63,7 @@
 
 
 def looks_kernel(
-    row_step, slots_ref, taps_ref, first_ref, second_ref, looks_ref, low_ref, high_ref, weight_ref, band_ref
+    row_step, firsts_ref, seconds_ref, taps_ref, first_ref, second_ref, looks_ref, low_ref, high_ref, weight_ref, band_ref
 ):
     rows, tiles = first_ref.shape[1], first_ref.shape[2]
     build_weights(taps_ref, weight_ref)
@@ -123,8 +125,9 @@
     high_ref[...] = looks_ref[:, :above].astype(jnp.bfloat16)
 
 
-def pair_looks(slots, taps, own, other):
-    dates, rows, tiles = own.shape[:3]
+def pair_looks(firsts, seconds, taps, own, other):
+    dates = firsts.shape[0]
+    rows, tiles = own.shape[1:3]
     row_step = 4
     tail = (4, tiles // 4, segments, lanes)
     image = (1, rows, tiles, segments, 2 * lanes)
@@ -136,32 +139,32 @@
             jax.ShapeDtypeStruct((dates, above) + tail, jnp.bfloat16),
         ),
         grid_spec=pltpu.PrefetchScalarGridSpec(
-            num_scalar_prefetch=1,
+            num_scalar_prefetch=2,
             grid=(dates,),
             in_specs=[
-                pl.BlockSpec((1, 2, lanes), lambda i, s: (i, 0, 0)),
-                pl.BlockSpec(image, lambda i, s: (i, 0, 0, 0, 0)),
-                pl.BlockSpec(image, lambda i, s: (s[i], 0, 0, 0, 0)),
+                pl.BlockSpec((1, 2, lanes), lambda i, f, s: (f[i], 0, 0)),
+                pl.BlockSpec(image, lambda i, f, s: (f[i], 0, 0, 0, 0)),
+                pl.BlockSpec(image, lambda i, f, s: (s[i], 0, 0, 0, 0)),
             ],
             out_specs=[
-                pl.BlockSpec((1, n) + tail, lambda i, s: (i, 0, 0, 0, 0, 0)) for n in (rows, below, above)
+                pl.BlockSpec((1, n) + tail, lambda i, f, s: (i, 0, 0, 0, 0, 0)) for n in (rows, below, above)
             ],
             scratch_shapes=[
                 pltpu.VMEM((2, 2 * lanes, 2 * lanes), jnp.bfloat16),
                 pltpu.VMEM((2, row_step, tiles, segments, 2 * lanes), jnp.bfloat16),
             ],
         ),
-        compiler_params=pltpu.CompilerParams(vmem_limit_bytes=40 << 20),
+        compiler_params=pltpu.CompilerParams(vmem_limit_bytes=14 << 20),
         cost_estimate=pl.CostEstimate(
             flops=dates * rows * tiles * segments * 2 * 2 * 512 * 256,
             bytes_accessed=dates * rows * tiles * segments * 256 * 8,
             transcendentals=0,
         ),
         name="looks",
-    )(slots, taps, own, other)
-
-
-def finish_kernel(looks_ref, low_ref, high_ref, *rest):
+    )(firsts, seconds, taps, own, other)
+
+
+def finish_kernel(places_ref, looks_ref, low_ref, high_ref, *rest):
     cross_ref, coherence_ref, turn_ref = rest[-3:]
     rows, halves = looks_ref.shape[1], looks_ref.shape[3]
     for a in range(halves):
@@ -192,11 +195,11 @@
             ].astype(jnp.bfloat16)
 
 
-def finish(match, looks, low, high, so_far):
-    dates, rows = looks.shape[:2]
+def finish(match, places, dates, looks, low, high, so_far):
+    count, rows = looks.shape[:2]
     tail = looks.shape[2:]
     columns = tail[1] * segments * lanes
-    block = lambda n: pl.BlockSpec((1, n) + tail, lambda i: (i, 0, 0, 0, 0, 0))
+    block = lambda n: pl.BlockSpec((1, n) + tail, lambda i, p: (i, 0, 0, 0, 0, 0))
     anywhere = pl.BlockSpec(memory_space=pl.ANY)
     return pl.pallas_call(
         finish_kernel,
@@ -204,41 +207,59 @@
             jax.ShapeDtypeStruct((2, dates, 2, rows, columns), jnp.bfloat16),
             jax.ShapeDtypeStruct((2, dates, rows, columns), jnp.bfloat16),
         ),
-        grid=(dates,),
-        in_specs=[block(rows), block(below), block(above)] + [anywhere] * len(so_far),
-        out_specs=[
-            pl.BlockSpec((1, 1, 2, rows, columns), lambda i: (match, i, 0, 0, 0)),
-            pl.BlockSpec((1, 1, rows, columns), lambda i: (match, i, 0, 0)),
-        ],
-        scratch_shapes=[pltpu.VMEM((3, segments * rows, lanes), jnp.float32)],
-        input_output_aliases={3 + i: i for i in range(len(so_far))},
-        compiler_params=pltpu.CompilerParams(vmem_limit_bytes=40 << 20),
+        grid_spec=pltpu.PrefetchScalarGridSpec(
+            num_scalar_prefetch=1,
+            grid=(count,),
+            in_specs=[block(rows), block(below), block(above)] + [anywhere] * len(so_far),
+            out_specs=[
+                pl.BlockSpec((1, 1, 2, rows, columns), lambda i, p: (match, p[i], 0, 0, 0)),
+                pl.BlockSpec((1, 1, rows, columns), lambda i, p: (match, p[i], 0, 0)),
+            ],
+            scratch_shapes=[pltpu.VMEM((3, segments * rows, lanes), jnp.float32)],
+        ),
+        input_output_aliases={4 + i: i for i in range(len(so_far))},
+        compiler_params=pltpu.CompilerParams(vmem_limit_bytes=10 << 20),
         cost_estimate=pl.CostEstimate(
-            flops=dates * rows * columns * 40, bytes_accessed=dates * rows * columns * 32, transcendentals=0
+            flops=count * rows * columns * 40, bytes_accessed=count * rows * columns * 32, transcendentals=0
         ),
         name="finish",
-    )(looks, low, high, *so_far)
+    )(places, looks, low, high, *so_far)
+
+
+def arrange(images):
+    dates, rows, _, samples = images.shape
+    tiles = samples // (segments * lanes)
+    images = images.reshape(dates, rows, 2, segments, tiles, lanes)
+    images = with_layout_constraint(images, Layout(major_to_minor=(0, 1, 3, 4, 2, 5)))
+    return images.transpose(0, 1, 4, 3, 2, 5).reshape(dates, rows, tiles, segments, 2 * lanes)
 
 
 def per_device(acquisitions, partners, band_shifts):
-    dates, rows, _, samples = acquisitions.shape
-    tiles = samples // (segments * lanes)
+    dates = acquisitions.shape[0]
     top_bit = lax.axis_size("date").bit_length() - 2
     strips = lax.axis_size("strip")
     upward = [(i, i + 1) for i in range(strips - 1)]
     downward = [(i + 1, i) for i in range(strips - 1)]
+    far = [partner(acquisitions[k : k + 1], "date", top_bit) for k in range(dates)]
     taps = make_taps(band_shifts)
     slots = partners % dates
-    own = acquisitions.reshape(dates, rows, 2, segments, tiles, lanes)
-    own = own.transpose(0, 1, 4, 3, 2, 5).reshape(dates, rows, tiles, segments, 2 * lanes)
-    far = partner(own, "date", top_bit)
+    every = jnp.arange(dates, dtype=jnp.int32)
+    own_of_slot = jnp.sum(jnp.where(slots[1][None, :] == every[:, None], every[None, :], 0), axis=1)
+    own = arrange(acquisitions)
     near = partner(own, "date", 0)
+
+    def halos(parts):
+        looks, low, high = parts
+        return looks, lax.ppermute(low, "strip", upward), lax.ppermute(high, "strip", downward)
+
+    pending = [(0, every) + halos(pair_looks(every, slots[0], taps[0], own, near))]
+    for k in range(dates):
+        place = own_of_slot[k : k + 1]
+        pair = pair_looks(place, jnp.zeros((1,), jnp.int32), taps[1], own, arrange(far[k]))
+        pending.append((1, place) + halos(pair))
     results = ()
-    for match, other in ((0, near), (1, far)):
-        looks, low, high = pair_looks(slots[match], taps[match], own, other)
-        low = lax.ppermute(low, "strip", upward)
-        high = lax.ppermute(high, "strip", downward)
-        results = finish(match, looks, low, high, results)
+    for match, place, looks, low, high in pending:
+        results = finish(match, place, dates, looks, low, high, results)
     return tuple(results)
 
 

time: 102 us -> 89.8 us (0.88)
  waiting for transfers between devices: 58.5 us -> 25.5 us
  local copies, waits for them, and re-layouts: 10.2 us -> 18.9 us
  Pallas kernels: 17.6 us -> 23.6 us
  starting transfers between devices: 14.3 us -> 20.2 us
    ppermute x2 -> x3, waiting for transfers between devices: 34 us -> 17.3 us  [partner(): return lax.ppermute(block, axis, route)]
    ppermute x4 -> x6, waiting for transfers between devices: 24.5 us -> 8.2 us  [the longest x3 8.19 us: halos(): lax.ppermute(high, 'strip', downward)]
    ppermute x4 -> x6, starting transfers between devices: 11.3 us -> 17.1 us  [the longest x3 13.2 us: halos(): lax.ppermute(low, 'strip', upward)]
    pallas_call x2 -> x3, Pallas kernels: 4.16 us -> 7.78 us  [finish(): pl.pallas_call(finish_kernel, out_shape=(jax.ShapeDtypeStruct((2, dates,...]
    unnamed x4 -> x16, local copies, waits for them, and re-layouts: 0.01 us -> 3.04 us
    slice x0 -> x2, local copies, waits for them, and re-layouts: none -> 2.92 us  [the longest x1 2.25 us: per_device(): acquisitions[k:k + 1]]
    reshape x3 -> x6, local copies, waits for them, and re-layouts: 10 us -> 12.7 us  [arrange(): images.transpose(0, 1, 4, 3, 2, 5)]
    pallas_call x2 -> x3, Pallas kernels: 13.5 us -> 15.8 us  [pair_looks(): pl.pallas_call(lambda *refs: looks_kernel(row_step, *refs), out_shape=(ja...]
  transfers between devices with their start and end apart: 6 -> 9, of which waited for: 4 -> 4; matrix products, arithmetic and copies ran while one was open for 0% -> 11% of each run, Pallas kernels for 15% -> 24%
where the time goes in v1:
time: 89.8 us; the launch traced here: 89.4 us
  waiting for transfers between devices  25.5 us (28%)
  Pallas kernels  23.6 us (26%)
  starting transfers between devices  20.2 us (22%)
  local copies, waits for them, and re-layouts  18.9 us (21%)
    ppermute x3, waiting for transfers between devices, partner(): return lax.ppermute(block, axis, route)  17.3 us
    pallas_call x3, Pallas kernels, pair_looks(): pl.pallas_call(lambda *refs: looks_kernel(row_step, *refs), out_shape=(ja...  15.8 us
    ppermute x3, starting transfers between devices, halos(): lax.ppermute(low, 'strip', upward)  13.2 us
    reshape x6, local copies, waits for them, and re-layouts, arrange(): images.transpose(0, 1, 4, 3, 2, 5)  12.7 us
    ppermute x3, waiting for transfers between devices, halos(): lax.ppermute(high, 'strip', downward)  8.19 us
    pallas_call x3, Pallas kernels, finish(): pl.pallas_call(finish_kernel, out_shape=(jax.ShapeDtypeStruct((2, dates,...  7.78 us
    ppermute x3, starting transfers between devices, halos(): lax.ppermute(high, 'strip', downward)  3.86 us
    ppermute x3, starting transfers between devices, partner(): return lax.ppermute(block, axis, route)  3.09 us
  transfers between devices with their start and end apart: 9, of which 4 were waited for; matrix products, arithmetic and copies ran while one was open for 11% of the time, Pallas kernels for 24%

profile of v1, /device:TPU:0, one launch (start us, length us, event | category | flops | bytes accessed | tf_op | source)
XLA Modules:
  0.0 89.4 jit_solution(15912066514094933681)
XLA Ops:
  0.6 4.4 %reshape.95 = bf16[2,16,8,16,256]{4,2,3,1,0:T(8,128)(2,1)} reshape(bf16[2,16,8,16,2,128]{5,4,2,3,1,0:T(2,128)(2,1)} %bitcast.24) | data formatting | bytes 4194304 | tf_op jit(solution)/shard_map/reshape | solution.py:234
  5.0 2.4 %copy.17.refs_3_ = bf16[2,16,8,16,256]{4,3,2,1,0:T(8,128)(2,1)S(1)} copy(bf16[2,16,8,16,256]{4,2,3,1,0:T(8,128)(2,1)} %reshape.95) | data formatting | bytes 4194304 | tf_op jit(solution)/shard_map/reshape | solution.py:234
  7.4 0.5 collective-permute-start.6
  8.0 2.2 %fusion.11 = (bf16[1,16,2,16384]{3,2,1,0:T(2,128)(2,1)S(1)}, bf16[1,16,2,16384]{3,2,1,0:T(2,128)(2,1)}) fusion(bf16[2,16,2,16384]{3,2,1,0:T(2,128)(2,1)S(1)} %copy-done.4), kind=kLoop, calls=%fused_computation.36 | loop fusion | bytes 4194304 | tf_op jit(solution)/shard_map/slice | solution.py:243
  10.2 2.5 %collective-permute-start.3 = (bf16[1,16,2,16384]{3,2,1,0:T(2,128)(2,1)S(1)}, bf16[1,16,2,16384]{3,2,1,0:T(2,128)(2,1)S(1)}, u32[]{:S(2)}, u32[]{:S(2)}) collective-permute-start(bf16[1,16,2,16384]{3,2,1,0:T(2,128)(2,1)S(1)} %get-tuple-element.28), channel_id=1, source_target_pairs={{0,8},{8,0},{4,12},{12,4},{1,9},{9,1},{5,13},{13,5},{2,10},{10,2},... | collective-permute-start | bytes 3145736 | tf_op jit(solution)/shard_map/ppermute | solution.py:28
  12.9 0.1 multiply_convert_fusion.1
  13.2 0.1 pad_maximum_fusion
  13.3 7.6 %looks.5 = (f32[2,16,4,2,16,128]{5,4,3,2,1,0:T(8,128)S(1)}, bf16[2,10,4,2,16,128]{5,4,3,2,1,0:T(8,128)(2,1)}, bf16[2,9,4,2,16,128]{5,4,3,2,1,0:T(8,128)(2,1)}) custom-call(s32[2]{0:T(128)S(1)} %iota.24.refs_0_, s32[2]{0:T(128)S(1)} %get-tuple-element.36.refs_1_, f32[2,2,128]{2,1,0:T(2,128)S(1)} %get-tuple-element.30.refs_2_, ...), custom_call_target="tpu_custom_call" | custom-call | flops 2147483648 | bytes 8388608 | tf_op jit(solution)/shard_map/looks/pallas_call | solution.py:134
  20.9 1.3 %copy-done = f32[2,16,4,2,16,128]{5,4,3,2,1,0:T(8,128)} copy-done((f32[2,16,4,2,16,128]{5,4,3,2,1,0:T(8,128)}, f32[2,16,4,2,16,128]{5,4,3,2,1,0:T(8,128)S(1)}, u32[]{:S(2)}) %copy-start) | copy-done | bytes 2097176
  22.2 1.3 %collective-permute-start.8 = (bf16[2,9,4,2,16,128]{5,4,3,2,1,0:T(8,128)(2,1)}, bf16[2,9,4,2,16,128]{5,4,3,2,1,0:T(8,128)(2,1)}, u32[]{:S(2)}, u32[]{:S(2)}) collective-permute-start(bf16[2,9,4,2,16,128]{5,4,3,2,1,0:T(8,128)(2,1)} %get-tuple-element.23), channel_id=1, source_target_pairs={{1,0},{2,1},{3,2},{5,4},{6,5},{7,6},{9,8},{10,9},{11,10},{13,12},{... | collective-permute-start | bytes 1769480 | tf_op jit(solution)/shard_map/ppermute | solution.py:253
  23.5 5.5 %collective-permute-start.7 = (bf16[2,10,4,2,16,128]{5,4,3,2,1,0:T(8,128)(2,1)}, bf16[2,10,4,2,16,128]{5,4,3,2,1,0:T(8,128)(2,1)}, u32[]{:S(2)}, u32[]{:S(2)}) collective-permute-start(bf16[2,10,4,2,16,128]{5,4,3,2,1,0:T(8,128)(2,1)} %get-tuple-element.22), channel_id=1, source_target_pairs={{0,1},{1,2},{2,3},{4,5},{5,6},{6,7},{8,9},{9,10},{10,11},{12,13},{... | collective-permute-start | bytes 1966088 | tf_op jit(solution)/shard_map/ppermute | solution.py:253
  29.0 0.1 fusion
  29.1 0.7 fusion.13
  29.8 6.9 %collective-permute-done.3 = bf16[1,16,2,16384]{3,2,1,0:T(2,128)(2,1)S(1)} collective-permute-done((bf16[1,16,2,16384]{3,2,1,0:T(2,128)(2,1)S(1)}, bf16[1,16,2,16384]{3,2,1,0:T(2,128)(2,1)S(1)}, u32[]{:S(2)}, u32[]{:S(2)}) %collective-permute-start.3) | collective-permute-done | bytes 1048608 | tf_op jit(solution)/shard_map/ppermute | solution.py:28
  36.7 1.0 %copy-done.5 = bf16[1,16,2,16384]{3,2,1,0:T(2,128)(2,1)} copy-done((bf16[1,16,2,16384]{3,2,1,0:T(2,128)(2,1)}, bf16[1,16,2,16384]{3,2,1,0:T(2,128)(2,1)S(1)}, u32[]{:S(2)}) %copy-start.5) | copy-done | bytes 1048600
  37.7 1.7 %reshape.97 = bf16[1,16,8,16,256]{4,2,3,1,0:T(8,128)(2,1)S(1)} reshape(bf16[1,16,8,16,2,128]{5,4,2,3,1,0:T(2,128)(2,1)} %bitcast.25) | data formatting | bytes 2097152 | tf_op jit(solution)/shard_map/reshape | solution.py:234
  39.5 0.2 copy.19.refs_4_
  39.7 4.3 %looks.4 = (f32[1,16,4,2,16,128]{5,4,3,2,1,0:T(8,128)S(1)}, bf16[1,10,4,2,16,128]{5,4,3,2,1,0:T(8,128)(2,1)}, bf16[1,9,4,2,16,128]{5,4,3,2,1,0:T(8,128)(2,1)S(1)}) custom-call(s32[1]{0:T(128)} %get-tuple-element.38.refs_0_.places_ref, s32[1]{0:T(128)} %constant.58.clone.1.refs_1_, f32[2,2,128]{2,1,0:T(2,128)S(1)} %get-tuple-element.31.refs_2_, ...), custom_call_target="tpu_custom_call" | custom-call | flops 1073741824 | bytes 4194304 | tf_op jit(solution)/shard_map/looks/pallas_call | solution.py:134
  44.1 0.7 copy-done.2
  44.8 4.0 %collective-permute-start.4 = (bf16[1,10,4,2,16,128]{5,4,3,2,1,0:T(8,128)(2,1)}, bf16[1,10,4,2,16,128]{5,4,3,2,1,0:T(8,128)(2,1)S(1)}, u32[]{:S(2)}, u32[]{:S(2)}) collective-permute-start(bf16[1,10,4,2,16,128]{5,4,3,2,1,0:T(8,128)(2,1)} %get-tuple-element.19), channel_id=1, source_target_pairs={{0,1},{1,2},{2,3},{4,5},{5,6},{6,7},{8,9},{9,10},{10,11},{12,13},{... | collective-permute-start | bytes 983048 | tf_op jit(solution)/shard_map/ppermute | solution.py:253
  48.7 10.4 %collective-permute-done = bf16[1,16,2,16384]{3,2,1,0:T(2,128)(2,1)} collective-permute-done((bf16[1,16,2,16384]{3,2,1,0:T(2,128)(2,1)}, bf16[1,16,2,16384]{3,2,1,0:T(2,128)(2,1)}, u32[]{:S(2)}, u32[]{:S(2)}) %collective-permute-start) | collective-permute-done | bytes 1048608 | tf_op jit(solution)/shard_map/ppermute | solution.py:28
  59.1 2.5 %reshape.96 = bf16[1,16,8,16,256]{4,2,3,1,0:T(8,128)(2,1)} reshape(bf16[1,16,8,16,2,128]{5,4,2,3,1,0:T(2,128)(2,1)} %bitcast.6) | data formatting | bytes 2097152 | tf_op jit(solution)/shard_map/reshape | solution.py:234
  61.6 1.5 %copy.18.refs_4_ = bf16[1,16,8,16,256]{4,3,2,1,0:T(8,128)(2,1)S(1)} copy(bf16[1,16,8,16,256]{4,2,3,1,0:T(8,128)(2,1)} %reshape.96) | data formatting | bytes 2097152 | tf_op jit(solution)/shard_map/reshape | solution.py:234
  63.1 3.9 %looks.3 = (f32[1,16,4,2,16,128]{5,4,3,2,1,0:T(8,128)S(1)}, bf16[1,10,4,2,16,128]{5,4,3,2,1,0:T(8,128)(2,1)S(1)}, bf16[1,9,4,2,16,128]{5,4,3,2,1,0:T(8,128)(2,1)S(1)}) custom-call(s32[1]{0:T(128)} %get-tuple-element.39.refs_0_.places_ref, s32[1]{0:T(128)} %constant.58.clone.1.refs_1_, f32[2,2,128]{2,1,0:T(2,128)S(1)} %get-tuple-element.31.refs_2_, ...), custom_call_target="tpu_custom_call" | custom-call | flops 1073741824 | bytes 4194304 | tf_op jit(solution)/shard_map/looks/pallas_call | solution.py:134
  67.0 3.7 %collective-permute-start.1 = (bf16[1,10,4,2,16,128]{5,4,3,2,1,0:T(8,128)(2,1)S(1)}, bf16[1,10,4,2,16,128]{5,4,3,2,1,0:T(8,128)(2,1)S(1)}, u32[]{:S(2)}, u32[]{:S(2)}) collective-permute-start(bf16[1,10,4,2,16,128]{5,4,3,2,1,0:T(8,128)(2,1)S(1)} %get-tuple-element.16), channel_id=1, source_target_pairs={{0,1},{1,2},{2,3},{4,5},{5,6},{6,7},{8,9},{9,10},{10,11},{12,13},{... | collective-permute-start | bytes 983048 | tf_op jit(solution)/shard_map/ppermute | solution.py:253
  70.8 1.3 %collective-permute-start.5 = (bf16[1,9,4,2,16,128]{5,4,3,2,1,0:T(8,128)(2,1)S(1)}, bf16[1,9,4,2,16,128]{5,4,3,2,1,0:T(8,128)(2,1)S(1)}, u32[]{:S(2)}, u32[]{:S(2)}) collective-permute-start(bf16[1,9,4,2,16,128]{5,4,3,2,1,0:T(8,128)(2,1)S(1)} %copy-done.3), channel_id=1, source_target_pairs={{1,0},{2,1},{3,2},{5,4},{6,5},{7,6},{9,8},{10,9},{11,10},{13,12},{... | collective-permute-start | bytes 884744 | tf_op jit(solution)/shard_map/ppermute | solution.py:253
  72.1 1.3 %collective-permute-start.2 = (bf16[1,9,4,2,16,128]{5,4,3,2,1,0:T(8,128)(2,1)S(1)}, bf16[1,9,4,2,16,128]{5,4,3,2,1,0:T(8,128)(2,1)S(1)}, u32[]{:S(2)}, u32[]{:S(2)}) collective-permute-start(bf16[1,9,4,2,16,128]{5,4,3,2,1,0:T(8,128)(2,1)S(1)} %get-tuple-element.17), channel_id=1, source_target_pairs={{1,0},{2,1},{3,2},{5,4},{6,5},{7,6},{9,8},{10,9},{11,10},{13,12},{... | collective-permute-start | bytes 884744 | tf_op jit(solution)/shard_map/ppermute | solution.py:253
  73.4 3.7 %finish.3 = (bf16[2,2,2,16,4096]{4,3,2,1,0:T(8,128)(2,1)}, bf16[2,2,16,4096]{3,2,1,0:T(8,128)(2,1)}) custom-call(s32[2]{0:T(128)S(1)} %iota.23.places_ref, f32[2,16,4,2,16,128]{5,4,3,2,1,0:T(8,128)S(1)} %copy-done.1, bf16[2,10,4,2,16,128]{5,4,3,2,1,0:T(8,128)(2,1)} %collective-permute-done.7.low_ref, ...), custom_call_target="tpu_custom_call" | custom-call | flops 5242880 | bytes 4194304 | tf_op jit(solution)/shard_map/finish/pallas_call | solution.py:204
  77.1 5.5 %collective-permute-done.5.high_ref = bf16[1,9,4,2,16,128]{5,4,3,2,1,0:T(8,128)(2,1)S(1)} collective-permute-done((bf16[1,9,4,2,16,128]{5,4,3,2,1,0:T(8,128)(2,1)S(1)}, bf16[1,9,4,2,16,128]{5,4,3,2,1,0:T(8,128)(2,1)S(1)}, u32[]{:S(2)}, u32[]{:S(2)}) %collective-permute-start.5) | collective-permute-done | bytes 294944 | tf_op jit(solution)/shard_map/ppermute | solution.py:253
  82.6 2.0 %finish.4 = (bf16[2,2,2,16,4096]{4,3,2,1,0:T(8,128)(2,1)}, bf16[2,2,16,4096]{3,2,1,0:T(8,128)(2,1)}) custom-call(s32[1]{0:T(128)} %get-tuple-element.38.refs_0_.places_ref, f32[1,16,4,2,16,128]{5,4,3,2,1,0:T(8,128)S(1)} %get-tuple-element.18.looks_ref, ...), custom_call_target="tpu_custom_call", output_to_operand_aliasing={{0}: (4, {}), {1}: (5, {})} | custom-call | flops 2621440 | bytes 2097152 | tf_op jit(solution)/shard_map/finish/pallas_call | solution.py:204
  84.6 2.7 %collective-permute-done.2.high_ref = bf16[1,9,4,2,16,128]{5,4,3,2,1,0:T(8,128)(2,1)S(1)} collective-permute-done((bf16[1,9,4,2,16,128]{5,4,3,2,1,0:T(8,128)(2,1)S(1)}, bf16[1,9,4,2,16,128]{5,4,3,2,1,0:T(8,128)(2,1)S(1)}, u32[]{:S(2)}, u32[]{:S(2)}) %collective-permute-start.2) | collective-permute-done | bytes 294944 | tf_op jit(solution)/shard_map/ppermute | solution.py:253
  87.3 2.1 %finish.5 = (bf16[2,2,2,16,4096]{4,3,2,1,0:T(8,128)(2,1)}, bf16[2,2,16,4096]{3,2,1,0:T(8,128)(2,1)}) custom-call(s32[1]{0:T(128)} %get-tuple-element.39.refs_0_.places_ref, f32[1,16,4,2,16,128]{5,4,3,2,1,0:T(8,128)S(1)} %get-tuple-element.15.looks_ref, ...), custom_call_target="tpu_custom_call", output_to_operand_aliasing={{0}: (4, {}), {1}: (5, {})} | custom-call | flops 2621440 | bytes 2097152 | tf_op jit(solution)/shard_map/finish/pallas_call | solution.py:204
  (32 shorter events, 0.3 us)
Async XLA Ops:
  5.0 2.9 %copy-start.4 = (bf16[2,16,2,16384]{3,2,1,0:T(2,128)(2,1)S(1)}, bf16[2,16,2,16384]{3,2,1,0:T(2,128)(2,1)}, u32[]{:S(2)}) copy-start(bf16[2,16,2,16384]{3,2,1,0:T(2,128)(2,1)} %param.3) | copy-start | bytes 6291460
  7.4 5.5 %copy-start.6 = (s32[2,2]{1,0:T(2,128)S(1)}, s32[2,2]{1,0:T(2,128)}, u32[]{:S(2)}) copy-start(s32[2,2]{1,0:T(2,128)} %param.5) | copy-start | bytes 52
  7.4 5.8 %copy-start.7 = (s32[2,2]{1,0:T(2,128)S(1)}, s32[2,2]{1,0:T(2,128)}, u32[]{:S(2)}) copy-start(s32[2,2]{1,0:T(2,128)} %param.4) | copy-start | bytes 52
  7.4 5.9 %collective-permute-start.6 = (bf16[2,16,8,16,256]{4,3,2,1,0:T(8,128)(2,1)S(1)}, bf16[2,16,8,16,256]{4,3,2,1,0:T(8,128)(2,1)S(1)}, u32[]{:S(2)}, u32[]{:S(2)}) collective-permute-start(bf16[2,16,8,16,256]{4,3,2,1,0:T(8,128)(2,1)S(1)} %copy.17.refs_3_), channel_id=1, source_target_pairs={{0,4},{4,0},{8,12},{12,8},{1,5},{5,1},{9,13},{13,9},{2,6},{6,2},{1... | collective-permute-start | bytes 6291464 | tf_op jit(solution)/shard_map/ppermute | solution.py:28
  10.2 26.5 %collective-permute-start.3 = (bf16[1,16,2,16384]{3,2,1,0:T(2,128)(2,1)S(1)}, bf16[1,16,2,16384]{3,2,1,0:T(2,128)(2,1)S(1)}, u32[]{:S(2)}, u32[]{:S(2)}) collective-permute-start(bf16[1,16,2,16384]{3,2,1,0:T(2,128)(2,1)S(1)} %get-tuple-element.28), channel_id=1, source_target_pairs={{0,8},{8,0},{4,12},{12,4},{1,9},{9,1},{5,13},{13,5},{2,10},{10,2},... | collective-permute-start | bytes 3145736 | tf_op jit(solution)/shard_map/ppermute | solution.py:28
  12.7 46.4 %collective-permute-start = (bf16[1,16,2,16384]{3,2,1,0:T(2,128)(2,1)}, bf16[1,16,2,16384]{3,2,1,0:T(2,128)(2,1)}, u32[]{:S(2)}, u32[]{:S(2)}) collective-permute-start(bf16[1,16,2,16384]{3,2,1,0:T(2,128)(2,1)} %get-tuple-element.29), channel_id=1, source_target_pairs={{0,8},{8,0},{4,12},{12,4},{1,9},{9,1},{5,13},{13,5},{2,10},{10,2},... | collective-permute-start | bytes 3145736 | tf_op jit(solution)/shard_map/ppermute | solution.py:28
  20.9 1.3 %copy-start = (f32[2,16,4,2,16,128]{5,4,3,2,1,0:T(8,128)}, f32[2,16,4,2,16,128]{5,4,3,2,1,0:T(8,128)S(1)}, u32[]{:S(2)}) copy-start(f32[2,16,4,2,16,128]{5,4,3,2,1,0:T(8,128)S(1)} %get-tuple-element.21.looks_ref) | copy-start | bytes 6291460
  22.2 49.9 %collective-permute-start.8 = (bf16[2,9,4,2,16,128]{5,4,3,2,1,0:T(8,128)(2,1)}, bf16[2,9,4,2,16,128]{5,4,3,2,1,0:T(8,128)(2,1)}, u32[]{:S(2)}, u32[]{:S(2)}) collective-permute-start(bf16[2,9,4,2,16,128]{5,4,3,2,1,0:T(8,128)(2,1)} %get-tuple-element.23), channel_id=1, source_target_pairs={{1,0},{2,1},{3,2},{5,4},{6,5},{7,6},{9,8},{10,9},{11,10},{13,12},{... | collective-permute-start | bytes 1769480 | tf_op jit(solution)/shard_map/ppermute | solution.py:253
  23.5 49.9 %collective-permute-start.7 = (bf16[2,10,4,2,16,128]{5,4,3,2,1,0:T(8,128)(2,1)}, bf16[2,10,4,2,16,128]{5,4,3,2,1,0:T(8,128)(2,1)}, u32[]{:S(2)}, u32[]{:S(2)}) collective-permute-start(bf16[2,10,4,2,16,128]{5,4,3,2,1,0:T(8,128)(2,1)} %get-tuple-element.22), channel_id=1, source_target_pairs={{0,1},{1,2},{2,3},{4,5},{5,6},{6,7},{8,9},{9,10},{10,11},{12,13},{... | collective-permute-start | bytes 1966088 | tf_op jit(solution)/shard_map/ppermute | solution.py:253
  36.7 1.0 %copy-start.5 = (bf16[1,16,2,16384]{3,2,1,0:T(2,128)(2,1)}, bf16[1,16,2,16384]{3,2,1,0:T(2,128)(2,1)S(1)}, u32[]{:S(2)}) copy-start(bf16[1,16,2,16384]{3,2,1,0:T(2,128)(2,1)S(1)} %collective-permute-done.3) | copy-start | bytes 3145732
  44.1 0.7 copy-start.2
  44.8 37.9 %collective-permute-start.4 = (bf16[1,10,4,2,16,128]{5,4,3,2,1,0:T(8,128)(2,1)}, bf16[1,10,4,2,16,128]{5,4,3,2,1,0:T(8,128)(2,1)S(1)}, u32[]{:S(2)}, u32[]{:S(2)}) collective-permute-start(bf16[1,10,4,2,16,128]{5,4,3,2,1,0:T(8,128)(2,1)} %get-tuple-element.19), channel_id=1, source_target_pairs={{0,1},{1,2},{2,3},{4,5},{5,6},{6,7},{8,9},{9,10},{10,11},{12,13},{... | collective-permute-start | bytes 983048 | tf_op jit(solution)/shard_map/ppermute | solution.py:253
  63.1 7.7 %copy-start.3 = (bf16[1,9,4,2,16,128]{5,4,3,2,1,0:T(8,128)(2,1)S(1)}, bf16[1,9,4,2,16,128]{5,4,3,2,1,0:T(8,128)(2,1)}, u32[]{:S(2)}) copy-start(bf16[1,9,4,2,16,128]{5,4,3,2,1,0:T(8,128)(2,1)} %copy-done.2) | copy-start | bytes 884740
  63.1 10.3 %copy-start.1 = (f32[2,16,4,2,16,128]{5,4,3,2,1,0:T(8,128)S(1)}, f32[2,16,4,2,16,128]{5,4,3,2,1,0:T(8,128)}, u32[]{:S(2)}) copy-start(f32[2,16,4,2,16,128]{5,4,3,2,1,0:T(8,128)} %copy-done) | copy-start | bytes 6291460
  67.0 20.3 %collective-permute-start.1 = (bf16[1,10,4,2,16,128]{5,4,3,2,1,0:T(8,128)(2,1)S(1)}, bf16[1,10,4,2,16,128]{5,4,3,2,1,0:T(8,128)(2,1)S(1)}, u32[]{:S(2)}, u32[]{:S(2)}) collective-permute-start(bf16[1,10,4,2,16,128]{5,4,3,2,1,0:T(8,128)(2,1)S(1)} %get-tuple-element.16), channel_id=1, source_target_pairs={{0,1},{1,2},{2,3},{4,5},{5,6},{6,7},{8,9},{9,10},{10,11},{12,13},{... | collective-permute-start | bytes 983048 | tf_op jit(solution)/shard_map/ppermute | solution.py:253
  70.8 11.8 %collective-permute-start.5 = (bf16[1,9,4,2,16,128]{5,4,3,2,1,0:T(8,128)(2,1)S(1)}, bf16[1,9,4,2,16,128]{5,4,3,2,1,0:T(8,128)(2,1)S(1)}, u32[]{:S(2)}, u32[]{:S(2)}) collective-permute-start(bf16[1,9,4,2,16,128]{5,4,3,2,1,0:T(8,128)(2,1)S(1)} %copy-done.3), channel_id=1, source_target_pairs={{1,0},{2,1},{3,2},{5,4},{6,5},{7,6},{9,8},{10,9},{11,10},{13,12},{... | collective-permute-start | bytes 884744 | tf_op jit(solution)/shard_map/ppermute | solution.py:253
  72.1 15.2 %collective-permute-start.2 = (bf16[1,9,4,2,16,128]{5,4,3,2,1,0:T(8,128)(2,1)S(1)}, bf16[1,9,4,2,16,128]{5,4,3,2,1,0:T(8,128)(2,1)S(1)}, u32[]{:S(2)}, u32[]{:S(2)}) collective-permute-start(bf16[1,9,4,2,16,128]{5,4,3,2,1,0:T(8,128)(2,1)S(1)} %get-tuple-element.17), channel_id=1, source_target_pairs={{1,0},{2,1},{3,2},{5,4},{6,5},{7,6},{9,8},{10,9},{11,10},{13,12},{... | collective-permute-start | bytes 884744 | tf_op jit(solution)/shard_map/ppermute | solution.py:253

commit v2 on v1

v2 whole, which is shorter than its diff:
```python
import math

import jax
import jax.numpy as jnp
from jax import lax
from jax.experimental import pallas as pl
from jax.experimental.layout import Layout, with_layout_constraint

from jax.experimental.pallas import tpu as pltpu
from jax.sharding import PartitionSpec as P

band_width = 0.8
bin_count = 256.0
epsilon = 1e-06
below = 10
above = 9
row_step = 2
in_flight = 3
lanes = 128
segments = 16


def make_taps(shift_bins):
    positions = jnp.arange(64, dtype=jnp.float32)
    centred = positions - 31.5
    hamming = 0.54 - 0.46 * jnp.cos(2.0 * math.pi * positions / 63.0)
    lowpass = hamming * band_width * jnp.sinc(band_width * centred)
    angles = 2.0 * math.pi * shift_bins.astype(jnp.float32)[..., None] * centred / bin_count
    taps = jnp.stack([lowpass * jnp.cos(angles), lowpass * jnp.sin(angles)], axis=-2)
    taps = taps.astype(jnp.bfloat16).astype(jnp.float32)
    zeros = jnp.zeros(taps.shape[:-1] + (64,), jnp.float32)
    return jnp.concatenate([taps[..., 32:], zeros, taps[..., :32]], axis=-1)


def circulant(row):
    block = jnp.broadcast_to(row, (32, lanes))
    parts = [pltpu.roll(block, phase, 1, stride=4, stride_axis=0) for phase in range(4)]
    return jnp.concatenate(parts, axis=0).T


def build_weights(taps_ref, weight_ref, spot):
    real_part = circulant(taps_ref[spot, 0:1, :])
    imag_part = circulant(taps_ref[spot, 1:2, :])
    k = lax.broadcasted_iota(jnp.int32, (lanes, lanes), 0)
    c = lax.broadcasted_iota(jnp.int32, (lanes, lanes), 1)
    t = 4 * (c & 31) + (c >> 5)
    inside = jnp.abs(k - t) < 64
    for place, mask in ((0, inside), (1, jnp.logical_not(inside))):
        re = jnp.where(mask, real_part, 0.0)
        im = jnp.where(mask, imag_part, 0.0)
        weight_ref[spot, place, 0:lanes, 0:lanes] = re.astype(jnp.bfloat16)
        weight_ref[spot, place, 0:lanes, lanes:] = im.astype(jnp.bfloat16)
        weight_ref[spot, place, lanes:, 0:lanes] = (-im).astype(jnp.bfloat16)
        weight_ref[spot, place, lanes:, lanes:] = re.astype(jnp.bfloat16)


def exchange_kernel(
    groups, strips, own_of_slot_ref, taps_ref, own_ref, looks_ref, low_ref, high_ref,
    got_ref, weight_ref, band_ref, low_out_ref, high_out_ref,
    got_send, got_recv, low_send, low_recv, high_send, high_recv,
):
    slots, rows, tiles = own_ref.shape[:3]
    chunks = rows // row_step
    low_first = (rows - below) // row_step
    high_last = (above - 1) // row_step
    me = lax.axis_index("date")
    strip = lax.axis_index("strip")
    peers = (me + 1 - 2 * lax.rem(me, 2), lax.rem(me + groups // 2, groups))
    can_up = strip < strips - 1
    can_down = strip > 0

    barrier = pltpu.get_barrier_semaphore()
    for peer in peers:
        pl.semaphore_signal(barrier, inc=1, device_id={"date": peer}, device_id_type=pl.DeviceIdType.MESH)

    @pl.when(can_up)
    def _():
        pl.semaphore_signal(barrier, inc=1, device_id={"strip": strip + 1}, device_id_type=pl.DeviceIdType.MESH)

    @pl.when(can_down)
    def _():
        pl.semaphore_signal(barrier, inc=1, device_id={"strip": strip - 1}, device_id_type=pl.DeviceIdType.MESH)

    pl.semaphore_wait(barrier, 2 + can_up.astype(jnp.int32) + can_down.astype(jnp.int32))

    def chunk_of(step):
        half = step // (chunks // 2)
        return (chunks - 1 - step) * (1 - half) + (step - chunks // 2) * half

    def date_copy(match, chunk):
        spot = pl.ds(chunk * row_step, row_step)
        return pltpu.make_async_remote_copy(
            src_ref=own_ref.at[:, spot],
            dst_ref=got_ref.at[match, :, spot],
            send_sem=got_send.at[match, chunk],
            recv_sem=got_recv.at[match, chunk],
            device_id={"date": peers[match]},
            device_id_type=pl.DeviceIdType.MESH,
        )

    def low_copy(match, chunk):
        spot = pl.ds((chunk - low_first) * row_step, row_step)
        return pltpu.make_async_remote_copy(
            src_ref=low_out_ref.at[match, spot],
            dst_ref=low_ref.at[match, spot],
            send_sem=low_send.at[match, chunk],
            recv_sem=low_recv.at[match, chunk],
            device_id={"strip": strip + 1},
            device_id_type=pl.DeviceIdType.MESH,
        )

    def high_copy(match, chunk):
        spot = pl.ds(chunk * row_step, row_step)
        return pltpu.make_async_remote_copy(
            src_ref=high_out_ref.at[match, spot],
            dst_ref=high_ref.at[match, spot],
            send_sem=high_send.at[match, chunk],
            recv_sem=high_recv.at[match, chunk],
            device_id={"strip": strip - 1},
            device_id_type=pl.DeviceIdType.MESH,
        )

    def start_dates(match):
        def body(step, carry):
            date_copy(match, chunk_of(step)).start()
            return carry

        return body

    lax.fori_loop(0, chunks, start_dates(0), 0)
    lax.fori_loop(0, in_flight, start_dates(1), 0)

    @pl.when(strip == 0)
    def _():
        low_ref[...] = jnp.zeros(low_ref.shape, low_ref.dtype)

    @pl.when(strip == strips - 1)
    def _():
        high_ref[...] = jnp.zeros(high_ref.shape, high_ref.dtype)

    def weigh(spot, carry):
        build_weights(taps_ref, weight_ref, spot)
        return carry

    lax.fori_loop(0, 2 * slots, weigh, 0)

    lane = lax.broadcasted_iota(jnp.int32, (segments, 2 * lanes), 1) & (lanes - 1)
    segment = lax.broadcasted_iota(jnp.int32, (segments, 2 * lanes), 0)
    from_before = jnp.where(lane >= 64, 1.0, 0.0).astype(jnp.bfloat16)
    from_after = jnp.where(lane < 64, 1.0, 0.0).astype(jnp.bfloat16)

    def filter_rows(load, spot, band):
        current, edges = [], []
        for i in range(row_step):
            x = [load(i, q) for q in range(tiles)]
            head = pltpu.roll(x[-1].astype(jnp.float32), 1, 0)
            head = jnp.where(segment == 0, 0.0, head).astype(jnp.bfloat16)
            tail = pltpu.roll(x[0].astype(jnp.float32), segments - 1, 0)
            tail = jnp.where(segment == segments - 1, 0.0, tail).astype(jnp.bfloat16)
            y = [head] + x + [tail]
            current += x
            edges += [y[q] * from_before + y[q + 2] * from_after for q in range(tiles)]
        current = jnp.concatenate(current, axis=0)
        edges = jnp.concatenate(edges, axis=0)
        out = jnp.dot(current, weight_ref[spot, 0], preferred_element_type=jnp.float32)
        out = out + jnp.dot(edges, weight_ref[spot, 1], preferred_element_type=jnp.float32)
        band_ref[band] = out.astype(jnp.bfloat16).reshape(row_step, tiles, segments, 2 * lanes)

    group = lax.broadcasted_iota(jnp.int32, (segments, lanes), 1) >> 5
    outer = (group == 0) | (group == 3)
    lower = group < 2
    even = (group & 1) == 0

    def pool(v):
        a = jnp.where(outer, v[0], v[2]) + pltpu.roll(jnp.where(outer, v[2], v[0]), 64, 1)
        b = jnp.where(lower, v[1], v[3]) + pltpu.roll(jnp.where(lower, v[3], v[1]), 64, 1)
        return jnp.where(even, a, b) + pltpu.roll(jnp.where(even, b, a), 32, 1)

    def run(match):
        def body(step, carry):
            chunk = chunk_of(step)
            start = chunk * row_step
            date_copy(match, chunk).wait_recv()
            if match == 1:
                date_copy(match, chunk).wait_send()

                @pl.when(step + in_flight < chunks)
                def _():
                    date_copy(match, chunk_of(step + in_flight)).start()

            for slot in range(slots):
                place = own_of_slot_ref[match, slot]
                spot = match * slots + slot
                filter_rows(lambda i, q: own_ref[place, start + i, q], spot, 2 * slot)
                filter_rows(lambda i, q: got_ref[match, slot, start + i, q], spot, 2 * slot + 1)
            for slot in range(slots):
                for i in range(row_step):
                    for a in range(tiles // 4):
                        planes = [[], [], [], []]
                        for b in range(4):
                            q = 4 * a + b
                            one = band_ref[2 * slot, i, q].astype(jnp.float32)
                            two = band_ref[2 * slot + 1, i, q].astype(jnp.float32)
                            fr, fi = one[:, :lanes], one[:, lanes:]
                            sr, si = two[:, :lanes], two[:, lanes:]
                            planes[0].append(fr * sr + fi * si)
                            planes[1].append(fi * sr - fr * si)
                            planes[2].append(fr * fr + fi * fi)
                            planes[3].append(sr * sr + si * si)
                        for p in range(4):
                            looks_ref[match, start + i, slot, p, a] = pool(planes[p])

            @pl.when((chunk >= low_first) & can_up)
            def _():
                low_out_ref[match, pl.ds((chunk - low_first) * row_step, row_step)] = looks_ref[
                    match, pl.ds(start, row_step)
                ].astype(jnp.bfloat16)
                low_copy(match, chunk).start()

            @pl.when((chunk <= high_last) & can_down)
            def _():
                high_out_ref[match, pl.ds(start, row_step)] = looks_ref[match, pl.ds(start, row_step)].astype(
                    jnp.bfloat16
                )
                high_copy(match, chunk).start()

            return carry

        return body

    for match in range(2):
        lax.fori_loop(0, chunks, run(match), 0)

    for match in range(2):

        def settle_low(chunk, carry):
            @pl.when(can_up)
            def _():
                low_copy(match, chunk).wait_send()

            @pl.when(can_down)
            def _():
                low_copy(match, chunk).wait_recv()

            return carry

        def settle_high(chunk, carry):
            @pl.when(can_down)
            def _():
                high_copy(match, chunk).wait_send()

            @pl.when(can_up)
            def _():
                high_copy(match, chunk).wait_recv()

            return carry

        lax.fori_loop(low_first, chunks, settle_low, 0)
        lax.fori_loop(0, high_last + 1, settle_high, 0)

    def settle_near(chunk, carry):
        date_copy(0, chunk).wait_send()
        return carry

    lax.fori_loop(0, chunks, settle_near, 0)


def exchange(own_of_slot, taps, own):
    slots, rows, tiles = own.shape[:3]
    chunks = rows // row_step
    groups, strips = lax.axis_size("date"), lax.axis_size("strip")
    tail = (slots, 4, tiles // 4, segments, lanes)
    high_rows = ((above - 1) // row_step + 1) * row_step
    in_vmem = pl.BlockSpec(memory_space=pltpu.VMEM)
    semaphores = pltpu.SemaphoreType.DMA((2, chunks))
    return pl.pallas_call(
        lambda *refs: exchange_kernel(groups, strips, *refs),
        out_shape=(
            jax.ShapeDtypeStruct((2, rows) + tail, jnp.float32),
            jax.ShapeDtypeStruct((2, below) + tail, jnp.bfloat16),
            jax.ShapeDtypeStruct((2, high_rows) + tail, jnp.bfloat16),
        ),
        in_specs=[pl.BlockSpec(memory_space=pltpu.SMEM), in_vmem, in_vmem],
        out_specs=[in_vmem] * 3,
        scratch_shapes=[
            pltpu.VMEM((2,) + own.shape, jnp.bfloat16),
            pltpu.VMEM((2 * slots, 2, 2 * lanes, 2 * lanes), jnp.bfloat16),
            pltpu.VMEM((2 * slots, row_step, tiles, segments, 2 * lanes), jnp.bfloat16),
            pltpu.VMEM((2, below) + tail, jnp.bfloat16),
            pltpu.VMEM((2, high_rows) + tail, jnp.bfloat16),
        ]
        + [semaphores] * 6,
        compiler_params=pltpu.CompilerParams(
            vmem_limit_bytes=36 << 20, collective_id=0, has_side_effects=True
        ),
        name="exchange",
    )(own_of_slot, taps, own)


def finish_kernel(places_ref, looks_ref, low_ref, high_ref, cross_ref, coherence_ref, turn_ref):
    rows, halves = looks_ref.shape[1], looks_ref.shape[4]
    for a in range(halves):
        for h in range(0, segments, 8):
            window = []
            for p in range(4):
                e = [low_ref[0, i, 0, p, a].astype(jnp.float32)[h : h + 8] for i in range(below)]
                e += [looks_ref[0, i, 0, p, a, h : h + 8, :] for i in range(rows)]
                e += [high_ref[0, i, 0, p, a].astype(jnp.float32)[h : h + 8] for i in range(above)]
                s2 = [e[i] + e[i + 1] for i in range(len(e) - 1)]
                s4 = [s2[i] + s2[i + 2] for i in range(len(s2) - 2)]
                s8 = [s4[i] + s4[i + 4] for i in range(len(s4) - 4)]
                window.append([s8[r] + s8[r + 8] + s4[r + 16] for r in range(rows)])
            for r in range(rows):
                cr, ci, pf, ps = (window[p][r] for p in range(4))
                spot = pl.ds(h * rows + r, 8, stride=rows)
                turn_ref[0, spot, :] = cr / 80.0
                turn_ref[1, spot, :] = ci / 80.0
                turn_ref[2, spot, :] = jnp.sqrt(cr * cr + ci * ci) * lax.rsqrt(pf * ps + epsilon)
        for s in range(segments):
            column = (s * halves + a) * lanes
            for k in range(2):
                cross_ref[0, 0, k, :, column : column + lanes] = turn_ref[
                    k, s * rows : (s + 1) * rows, :
                ].astype(jnp.bfloat16)
            coherence_ref[0, 0, :, column : column + lanes] = turn_ref[
                2, s * rows : (s + 1) * rows, :
            ].astype(jnp.bfloat16)


def finish(places, looks, low, high):
    matches, rows, dates = looks.shape[:3]
    tail = looks.shape[3:]
    columns = tail[1] * segments * lanes
    block = lambda n: pl.BlockSpec((1, n, 1) + tail, lambda m, i, p: (m, 0, i, 0, 0, 0, 0))
    return pl.pallas_call(
        finish_kernel,
        out_shape=(
            jax.ShapeDtypeStruct((matches, dates, 2, rows, columns), jnp.bfloat16),
            jax.ShapeDtypeStruct((matches, dates, rows, columns), jnp.bfloat16),
        ),
        grid_spec=pltpu.PrefetchScalarGridSpec(
            num_scalar_prefetch=1,
            grid=(matches, dates),
            in_specs=[block(rows), block(low.shape[1]), block(high.shape[1])],
            out_specs=[
                pl.BlockSpec((1, 1, 2, rows, columns), lambda m, i, p: (m, p[m, i], 0, 0, 0)),
                pl.BlockSpec((1, 1, rows, columns), lambda m, i, p: (m, p[m, i], 0, 0)),
            ],
            scratch_shapes=[pltpu.VMEM((3, segments * rows, lanes), jnp.float32)],
        ),
        compiler_params=pltpu.CompilerParams(vmem_limit_bytes=10 << 20),
        name="finish",
    )(places, looks, low, high)


def arrange(images):
    dates, rows, _, samples = images.shape
    tiles = samples // (segments * lanes)
    images = images.reshape(dates, rows, 2, segments, tiles, lanes)
    images = with_layout_constraint(images, Layout(major_to_minor=(0, 1, 3, 4, 2, 5)))
    return images.transpose(0, 1, 4, 3, 2, 5).reshape(dates, rows, tiles, segments, 2 * lanes)


def per_device(acquisitions, partners, band_shifts):
    dates = acquisitions.shape[0]
    slots = partners % dates
    every = jnp.arange(dates, dtype=jnp.int32)
    met = slots[:, None, :] == every[None, :, None]
    own_of_slot = jnp.sum(jnp.where(met, every[None, None, :], 0), axis=2)
    shifts = jnp.sum(jnp.where(met, band_shifts[:, None, :], 0), axis=2)
    taps = make_taps(shifts).reshape(2 * dates, 2, lanes)
    looks, low, high = exchange(own_of_slot, taps, arrange(acquisitions))
    return finish(own_of_slot, looks, low, high)


def solution(mesh):
    in_specs = (
        P(("grp", "date"), "strip", None, None),
        P(None, ("grp", "date")),
        P(None, ("grp", "date")),
    )
    out_specs = (
        P(None, ("grp", "date"), None, "strip", None),
        P(None, ("grp", "date"), "strip", None),
    )
    return jax.shard_map(
        per_device, mesh=mesh, in_specs=in_specs, out_specs=out_specs, check_vma=False
    )
```

time: 89.8 us -> 67.7 us (0.75)
  Pallas kernels: 23.6 us -> 61.1 us
  waiting for transfers between devices: 25.5 us -> 0 us
  starting transfers between devices: 20.2 us -> 0 us
  local copies, waits for them, and re-layouts: 18.9 us -> 3.95 us
  other arithmetic: 0.42 us -> 1.77 us
    pallas_call x6 -> x2, Pallas kernels: 23.6 us -> 61.1 us  [the longest x1 56.5 us: exchange(): pl.pallas_call(lambda *refs: exchange_kernel(groups, strips, *refs), out_...]
    ppermute x9 -> x0, waiting for transfers between devices: 25.5 us -> none  [the longest x3 17.3 us: partner(): return lax.ppermute(block, axis, route)]
    ppermute x9 -> x0, starting transfers between devices: 20.2 us -> none  [the longest x3 13.2 us: halos(): lax.ppermute(low, 'strip', upward)]
    reshape x6 -> x2, local copies, waits for them, and re-layouts: 12.7 us -> 3.79 us  [arrange(): images.transpose(0, 1, 4, 3, 2, 5)]
    unnamed x16 -> x0, local copies, waits for them, and re-layouts: 3.04 us -> none
    slice x2 -> x0, local copies, waits for them, and re-layouts: 2.92 us -> none  [the longest x1 2.25 us: per_device(): acquisitions[k:k + 1]]
  transfers between devices with their start and end apart: 9 -> 0, of which waited for: 4 -> 0; matrix products, arithmetic and copies ran while one was open for 11% -> 0% of each run, Pallas kernels for 24% -> 0%
where the time goes in v2:
time: 67.7 us; the launch traced here: 67.5 us
  Pallas kernels  61.1 us (90%)
  local copies, waits for them, and re-layouts  3.95 us (6%)
  other arithmetic  1.77 us (3%)
  between operations  0.69 us (1%)
    pallas_call x1, Pallas kernels, exchange(): pl.pallas_call(lambda *refs: exchange_kernel(groups, strips, *refs), out_...  56.5 us
    pallas_call x1, Pallas kernels, finish(): pl.pallas_call(finish_kernel, out_shape=(jax.ShapeDtypeStruct((matches, d...  4.59 us
    reshape x2, local copies, waits for them, and re-layouts, arrange(): images.transpose(0, 1, 4, 3, 2, 5)  3.79 us

profile of v2, /device:TPU:0, one launch (start us, length us, event | category | flops | bytes accessed | tf_op | source)
XLA Modules:
  0.0 67.5 jit_solution(2642236632210905611)
XLA Ops:
  0.6 0.1 pad.1.clone
  0.7 0.7 %and_select_fusion = s32[2,2]{1,0:T(2,128)S(1)} fusion(s32[2,2]{1,0:T(2,128)} %param.4), kind=kLoop, calls=%fused_computation.13 | loop fusion | flops 44 | bytes 32 | tf_op jit(solution)/shard_map/jit(remainder)/select_n | solution.py:366
  1.4 0.8 %select_reduce_fusion = (s32[2,2]{1,0:T(2,128)S(1)}, s32[2,2]{1,0:T(2,128)S(1)}) fusion(s32[2,2]{1,0:T(2,128)} %param.5, s32[2,2]{1,0:T(2,128)S(1)} %and_select_fusion), kind=kLoop, calls=%fused_computation.7 | loop fusion | flops 32 | bytes 64 | tf_op jit(solution)/shard_map/reduce_sum | solution.py:370
  2.2 0.1 iota_add_fusion
  2.3 0.1 multiply_convert_fusion.1
  2.4 0.1 fusion.10
  2.5 0.1 pad_maximum_fusion
  2.6 3.2 %reshape.88 = bf16[2,16,8,16,256]{4,2,3,1,0:T(8,128)(2,1)S(1)} reshape(bf16[2,16,8,16,2,128]{5,4,2,3,1,0:T(2,128)(2,1)} %bitcast.7) | data formatting | bytes 4194304 | tf_op jit(solution)/shard_map/reshape | solution.py:361
  5.8 0.6 copy.10.refs_2_
  6.4 56.5 %exchange.1 = (f32[2,16,2,4,2,16,128]{6,5,4,3,2,1,0:T(8,128)S(1)}, bf16[2,10,2,4,2,16,128]{6,5,4,3,2,1,0:T(8,128)(2,1)S(1)}, bf16[2,10,2,4,2,16,128]{6,5,4,3,2,1,0:T(8,128)(2,1)S(1)}) custom-call(s32[2,2]{1,0:T(2,128)S(1)} %get-tuple-element.9.refs_0_.places_ref, f32[4,2,128]{2,1,0:T(2,128)S(1)} %bitcast.6, bf16[2,16,8,16,256]{4,3,2,1,0:T(8,128)(2,1)S(1)} %copy.10.refs_2_), custom_call_target="tpu_custom_call" | custom-call | tf_op jit(solution)/shard_map/exchange/pallas_call | solution.py:276
  62.9 4.6 %finish.1 = (bf16[2,2,2,16,4096]{4,3,2,1,0:T(8,128)(2,1)}, bf16[2,2,16,4096]{3,2,1,0:T(8,128)(2,1)}) custom-call(s32[2,2]{1,0:T(2,128)S(1)} %get-tuple-element.9.refs_0_.places_ref, f32[2,16,2,4,2,16,128]{6,5,4,3,2,1,0:T(8,128)S(1)} %get-tuple-element.5.looks_ref, bf16[2,10,2,4,2,16,128]{6,5,4,3,2,1,0:T(8,128)(2,1)S(1)} %get-tuple-element.6.low_ref, ...), custom_call_target="tpu_custom_call" | custom-call | tf_op jit(solution)/shard_map/finish/pallas_call | solution.py:335
  (5 shorter events, 0.0 us)

commit v3 on v2

--- a/solution.py
+++ b/solution.py
@@ -38,9 +38,16 @@
     return jnp.concatenate(parts, axis=0).T
 
 
-def build_weights(taps_ref, weight_ref, spot):
-    real_part = circulant(taps_ref[spot, 0:1, :])
-    imag_part = circulant(taps_ref[spot, 1:2, :])
+def place_of(partners_ref, match, slot, dates):
+    place = 0
+    for i in range(1, dates):
+        place = place + jnp.where(lax.rem(partners_ref[match, i], dates) == slot, i, 0)
+    return place
+
+
+def build_weights(taps_ref, weight_ref, spot, source):
+    real_part = circulant(taps_ref[source, 0:1, :])
+    imag_part = circulant(taps_ref[source, 1:2, :])
     k = lax.broadcasted_iota(jnp.int32, (lanes, lanes), 0)
     c = lax.broadcasted_iota(jnp.int32, (lanes, lanes), 1)
     t = 4 * (c & 31) + (c >> 5)
@@ -55,7 +62,7 @@
 
 
 def exchange_kernel(
-    groups, strips, own_of_slot_ref, taps_ref, own_ref, looks_ref, low_ref, high_ref,
+    groups, strips, partners_ref, taps_ref, own_ref, looks_ref, low_ref, high_ref,
     got_ref, weight_ref, band_ref, low_out_ref, high_out_ref,
     got_send, got_recv, low_send, low_recv, high_send, high_recv,
 ):
@@ -127,8 +134,8 @@
 
         return body
 
+    lax.fori_loop(0, in_flight, start_dates(1), 0)
     lax.fori_loop(0, chunks, start_dates(0), 0)
-    lax.fori_loop(0, in_flight, start_dates(1), 0)
 
     @pl.when(strip == 0)
     def _():
@@ -139,7 +146,9 @@
         high_ref[...] = jnp.zeros(high_ref.shape, high_ref.dtype)
 
     def weigh(spot, carry):
-        build_weights(taps_ref, weight_ref, spot)
+        match = spot // slots
+        place = place_of(partners_ref, match, lax.rem(spot, slots), slots)
+        build_weights(taps_ref, weight_ref, spot, match * slots + place)
         return carry
 
     lax.fori_loop(0, 2 * slots, weigh, 0)
@@ -189,7 +198,7 @@
                     date_copy(match, chunk_of(step + in_flight)).start()
 
             for slot in range(slots):
-                place = own_of_slot_ref[match, slot]
+                place = place_of(partners_ref, match, slot, slots)
                 spot = match * slots + slot
                 filter_rows(lambda i, q: own_ref[place, start + i, q], spot, 2 * slot)
                 filter_rows(lambda i, q: got_ref[match, slot, start + i, q], spot, 2 * slot + 1)
@@ -265,7 +274,7 @@
     lax.fori_loop(0, chunks, settle_near, 0)
 
 
-def exchange(own_of_slot, taps, own):
+def exchange(partners, taps, own):
     slots, rows, tiles = own.shape[:3]
     chunks = rows // row_step
     groups, strips = lax.axis_size("date"), lax.axis_size("strip")
@@ -294,7 +303,7 @@
             vmem_limit_bytes=36 << 20, collective_id=0, has_side_effects=True
         ),
         name="exchange",
-    )(own_of_slot, taps, own)
+    )(partners, taps, own)
 
 
 def finish_kernel(places_ref, looks_ref, low_ref, high_ref, cross_ref, coherence_ref, turn_ref):
@@ -343,8 +352,8 @@
             grid=(matches, dates),
             in_specs=[block(rows), block(low.shape[1]), block(high.shape[1])],
             out_specs=[
-                pl.BlockSpec((1, 1, 2, rows, columns), lambda m, i, p: (m, p[m, i], 0, 0, 0)),
-                pl.BlockSpec((1, 1, rows, columns), lambda m, i, p: (m, p[m, i], 0, 0)),
+                pl.BlockSpec((1, 1, 2, rows, columns), lambda m, i, p: (m, place_of(p, m, i, dates), 0, 0, 0)),
+                pl.BlockSpec((1, 1, rows, columns), lambda m, i, p: (m, place_of(p, m, i, dates), 0, 0)),
             ],
             scratch_shapes=[pltpu.VMEM((3, segments * rows, lanes), jnp.float32)],
         ),
@@ -363,14 +372,9 @@
 
 def per_device(acquisitions, partners, band_shifts):
     dates = acquisitions.shape[0]
-    slots = partners % dates
-    every = jnp.arange(dates, dtype=jnp.int32)
-    met = slots[:, None, :] == every[None, :, None]
-    own_of_slot = jnp.sum(jnp.where(met, every[None, None, :], 0), axis=2)
-    shifts = jnp.sum(jnp.where(met, band_shifts[:, None, :], 0), axis=2)
-    taps = make_taps(shifts).reshape(2 * dates, 2, lanes)
-    looks, low, high = exchange(own_of_slot, taps, arrange(acquisitions))
-    return finish(own_of_slot, looks, low, high)
+    taps = make_taps(band_shifts).reshape(2 * dates, 2, lanes)
+    looks, low, high = exchange(partners, taps, arrange(acquisitions))
+    return finish(partners, looks, low, high)
 
 
 def solution(mesh):

time: 67.7 us -> 67 us (0.990)
  other arithmetic: 1.77 us -> 0.94 us
    reduce_sum x1 -> x0, other arithmetic: 0.82 us -> none  [per_device(): shifts = jnp.sum(jnp.where(met, band_shifts[:, None, :], 0), axis=2)]
    select_n x1 -> x0, other arithmetic: 0.69 us -> none  [per_device(): slots = partners % dates]
where the time goes in v3:
time: 67 us; the launch traced here: 66.8 us
  Pallas kernels  61.2 us (91%)
  local copies, waits for them, and re-layouts  3.98 us (6%)
  other arithmetic  0.94 us (1%)
  between operations  0.68 us (1%)
    pallas_call x1, Pallas kernels, exchange(): pl.pallas_call(lambda *refs: exchange_kernel(groups, strips, *refs), out_...  56.5 us
    pallas_call x1, Pallas kernels, finish(): pl.pallas_call(finish_kernel, out_shape=(jax.ShapeDtypeStruct((matches, d...  4.65 us
    reshape x2, local copies, waits for them, and re-layouts, arrange(): images.transpose(0, 1, 4, 3, 2, 5)  3.79 us

profile of v3, /device:TPU:0, one launch (start us, length us, event | category | flops | bytes accessed | tf_op | source)
XLA Modules:
  0.0 66.8 jit_solution(7112086437497359341)
XLA Ops:
  0.6 0.1 pad.1.clone
  0.7 0.7 %convert_multiply_fusion = f32[2,2]{1,0:T(2,128)S(1)} fusion(s32[2,2]{1,0:T(2,128)} %param.5), kind=kLoop, calls=%fused_computation.10 | loop fusion | flops 8 | bytes 32 | tf_op jit(solution)/shard_map/mul | solution.py:28
  1.4 0.1 iota_add_fusion
  1.4 0.1 multiply_convert_fusion.1
  1.6 0.1 fusion.9
  1.7 0.1 pad_maximum_fusion
  1.8 3.2 %reshape.83 = bf16[2,16,8,16,256]{4,2,3,1,0:T(8,128)(2,1)S(1)} reshape(bf16[2,16,8,16,2,128]{5,4,2,3,1,0:T(2,128)(2,1)} %bitcast.7) | data formatting | bytes 4194304 | tf_op jit(solution)/shard_map/reshape | solution.py:370
  4.9 0.0 copy-start
  4.9 0.6 copy.9.refs_2_
  5.6 0.0 copy-done
  5.6 56.5 %exchange.1 = (f32[2,16,2,4,2,16,128]{6,5,4,3,2,1,0:T(8,128)S(1)}, bf16[2,10,2,4,2,16,128]{6,5,4,3,2,1,0:T(8,128)(2,1)S(1)}, bf16[2,10,2,4,2,16,128]{6,5,4,3,2,1,0:T(8,128)(2,1)S(1)}) custom-call(s32[2,2]{1,0:T(2,128)S(1)} %copy-done, f32[4,2,128]{2,1,0:T(2,128)S(1)} %bitcast.6, bf16[2,16,8,16,256]{4,3,2,1,0:T(8,128)(2,1)S(1)} %copy.9.refs_2_), custom_call_target="tpu_custom_call" | custom-call | tf_op jit(solution)/shard_map/exchange/pallas_call | solution.py:285
  62.1 4.6 %finish.1 = (bf16[2,2,2,16,4096]{4,3,2,1,0:T(8,128)(2,1)}, bf16[2,2,16,4096]{3,2,1,0:T(8,128)(2,1)}) custom-call(s32[2,2]{1,0:T(2,128)S(1)} %copy-done, f32[2,16,2,4,2,16,128]{6,5,4,3,2,1,0:T(8,128)S(1)} %get-tuple-element.5.looks_ref, bf16[2,10,2,4,2,16,128]{6,5,4,3,2,1,0:T(8,128)(2,1)S(1)} %get-tuple-element.6.low_ref, ...), custom_call_target="tpu_custom_call" | custom-call | tf_op jit(solution)/shard_map/finish/pallas_call | solution.py:344
  (4 shorter events, 0.0 us)
Async XLA Ops:
  4.9 0.7 %copy-start = (s32[2,2]{1,0:T(2,128)S(1)}, s32[2,2]{1,0:T(2,128)}, u32[]{:S(2)}) copy-start(s32[2,2]{1,0:T(2,128)} %places_ref.1) | copy-start | bytes 52

commit v4 on v3

--- a/solution.py
+++ b/solution.py
@@ -62,8 +62,8 @@
 
 
 def exchange_kernel(
-    groups, strips, partners_ref, taps_ref, own_ref, looks_ref, low_ref, high_ref,
-    got_ref, weight_ref, band_ref, low_out_ref, high_out_ref,
+    groups, strips, partners_ref, taps_ref, own_ref, looks_ref, low_ref, high_ref, made_ref,
+    turn_ref, got_ref, weight_ref, band_ref, low_out_ref, high_out_ref,
     got_send, got_recv, low_send, low_recv, high_send, high_recv,
 ):
     slots, rows, tiles = own_ref.shape[:3]
@@ -237,11 +237,7 @@
 
         return body
 
-    for match in range(2):
-        lax.fori_loop(0, chunks, run(match), 0)
-
-    for match in range(2):
-
+    def settle(match):
         def settle_low(chunk, carry):
             @pl.when(can_up)
             def _():
@@ -266,6 +262,32 @@
 
         lax.fori_loop(low_first, chunks, settle_low, 0)
         lax.fori_loop(0, high_last + 1, settle_high, 0)
+
+    def make_first(slot, carry):
+        def store_cross(k, column, value):
+            made_ref[slot, k, :, column] = value
+
+        def store_coherence(column, value):
+            made_ref[slot, 2, :, column] = value
+
+        window_rows(
+            lambda i, p, a: low_ref[0, i, slot, p, a],
+            lambda i, p, a, h: looks_ref[0, i, slot, p, a, h : h + 8, :],
+            lambda i, p, a: high_ref[0, i, slot, p, a],
+            store_cross,
+            store_coherence,
+            turn_ref,
+            rows,
+            tiles // 4,
+        )
+        return carry
+
+    lax.fori_loop(0, chunks, run(0), 0)
+    lax.fori_loop(0, chunks - 3, run(1), 0)
+    settle(0)
+    lax.fori_loop(0, slots, make_first, 0)
+    lax.fori_loop(chunks - 3, chunks, run(1), 0)
+    settle(1)
 
     def settle_near(chunk, carry):
         date_copy(0, chunk).wait_send()
@@ -288,10 +310,12 @@
             jax.ShapeDtypeStruct((2, rows) + tail, jnp.float32),
             jax.ShapeDtypeStruct((2, below) + tail, jnp.bfloat16),
             jax.ShapeDtypeStruct((2, high_rows) + tail, jnp.bfloat16),
+            jax.ShapeDtypeStruct((slots, 3, rows, tail[2] * segments * lanes), jnp.bfloat16),
         ),
         in_specs=[pl.BlockSpec(memory_space=pltpu.SMEM), in_vmem, in_vmem],
-        out_specs=[in_vmem] * 3,
+        out_specs=[in_vmem] * 4,
         scratch_shapes=[
+            pltpu.VMEM((3, segments * rows, lanes), jnp.float32),
             pltpu.VMEM((2,) + own.shape, jnp.bfloat16),
             pltpu.VMEM((2 * slots, 2, 2 * lanes, 2 * lanes), jnp.bfloat16),
             pltpu.VMEM((2 * slots, row_step, tiles, segments, 2 * lanes), jnp.bfloat16),
@@ -306,15 +330,14 @@
     )(partners, taps, own)
 
 
-def finish_kernel(places_ref, looks_ref, low_ref, high_ref, cross_ref, coherence_ref, turn_ref):
-    rows, halves = looks_ref.shape[1], looks_ref.shape[4]
+def window_rows(load_low, load_looks, load_high, store_cross, store_coherence, turn_ref, rows, halves):
     for a in range(halves):
         for h in range(0, segments, 8):
             window = []
             for p in range(4):
-                e = [low_ref[0, i, 0, p, a].astype(jnp.float32)[h : h + 8] for i in range(below)]
-                e += [looks_ref[0, i, 0, p, a, h : h + 8, :] for i in range(rows)]
-                e += [high_ref[0, i, 0, p, a].astype(jnp.float32)[h : h + 8] for i in range(above)]
+                e = [load_low(i, p, a).astype(jnp.float32)[h : h + 8] for i in range(below)]
+                e += [load_looks(i, p, a, h) for i in range(rows)]
+                e += [load_high(i, p, a).astype(jnp.float32)[h : h + 8] for i in range(above)]
                 s2 = [e[i] + e[i + 1] for i in range(len(e) - 1)]
                 s4 = [s2[i] + s2[i + 2] for i in range(len(s2) - 2)]
                 s8 = [s4[i] + s4[i + 4] for i in range(len(s4) - 4)]
@@ -326,21 +349,45 @@
                 turn_ref[1, spot, :] = ci / 80.0
                 turn_ref[2, spot, :] = jnp.sqrt(cr * cr + ci * ci) * lax.rsqrt(pf * ps + epsilon)
         for s in range(segments):
-            column = (s * halves + a) * lanes
+            column = slice((s * halves + a) * lanes, (s * halves + a + 1) * lanes)
             for k in range(2):
-                cross_ref[0, 0, k, :, column : column + lanes] = turn_ref[
-                    k, s * rows : (s + 1) * rows, :
-                ].astype(jnp.bfloat16)
-            coherence_ref[0, 0, :, column : column + lanes] = turn_ref[
-                2, s * rows : (s + 1) * rows, :
-            ].astype(jnp.bfloat16)
-
-
-def finish(places, looks, low, high):
+                store_cross(k, column, turn_ref[k, s * rows : (s + 1) * rows, :].astype(jnp.bfloat16))
+            store_coherence(column, turn_ref[2, s * rows : (s + 1) * rows, :].astype(jnp.bfloat16))
+
+
+def finish_kernel(places_ref, looks_ref, low_ref, high_ref, made_ref, cross_ref, coherence_ref, turn_ref):
+    rows, halves = looks_ref.shape[1], looks_ref.shape[4]
+
+    @pl.when(pl.program_id(0) == 0)
+    def _():
+        cross_ref[0, 0] = made_ref[0, 0:2]
+        coherence_ref[0, 0] = made_ref[0, 2]
+
+    @pl.when(pl.program_id(0) == 1)
+    def _():
+        def store_cross(k, column, value):
+            cross_ref[0, 0, k, :, column] = value
+
+        def store_coherence(column, value):
+            coherence_ref[0, 0, :, column] = value
+
+        window_rows(
+            lambda i, p, a: low_ref[0, i, 0, p, a],
+            lambda i, p, a, h: looks_ref[0, i, 0, p, a, h : h + 8, :],
+            lambda i, p, a: high_ref[0, i, 0, p, a],
+            store_cross,
+            store_coherence,
+            turn_ref,
+            rows,
+            halves,
+        )
+
+
+def finish(places, looks, low, high, made):
     matches, rows, dates = looks.shape[:3]
     tail = looks.shape[3:]
     columns = tail[1] * segments * lanes
-    block = lambda n: pl.BlockSpec((1, n, 1) + tail, lambda m, i, p: (m, 0, i, 0, 0, 0, 0))
+    block = lambda n: pl.BlockSpec((1, n, 1) + tail, lambda m, i, p: (1, 0, i * m, 0, 0, 0, 0))
     return pl.pallas_call(
         finish_kernel,
         out_shape=(
@@ -350,7 +397,8 @@
         grid_spec=pltpu.PrefetchScalarGridSpec(
             num_scalar_prefetch=1,
             grid=(matches, dates),
-            in_specs=[block(rows), block(low.shape[1]), block(high.shape[1])],
+            in_specs=[block(rows), block(low.shape[1]), block(high.shape[1]),
+                pl.BlockSpec((1, 3, rows, columns), lambda m, i, p: (i * (1 - m) + (dates - 1) * m, 0, 0, 0))],
             out_specs=[
                 pl.BlockSpec((1, 1, 2, rows, columns), lambda m, i, p: (m, place_of(p, m, i, dates), 0, 0, 0)),
                 pl.BlockSpec((1, 1, rows, columns), lambda m, i, p: (m, place_of(p, m, i, dates), 0, 0)),
@@ -359,7 +407,7 @@
         ),
         compiler_params=pltpu.CompilerParams(vmem_limit_bytes=10 << 20),
         name="finish",
-    )(places, looks, low, high)
+    )(places, looks, low, high, made)
 
 
 def arrange(images):
@@ -373,8 +421,8 @@
 def per_device(acquisitions, partners, band_shifts):
     dates = acquisitions.shape[0]
     taps = make_taps(band_shifts).reshape(2 * dates, 2, lanes)
-    looks, low, high = exchange(partners, taps, arrange(acquisitions))
-    return finish(partners, looks, low, high)
+    looks, low, high, made = exchange(partners, taps, arrange(acquisitions))
+    return finish(partners, looks, low, high, made)
 
 
 def solution(mesh):

time: 67 us -> 66.2 us (0.988)
  Pallas kernels: 61.2 us -> 60.4 us
    pallas_call x1, Pallas kernels: 4.65 us -> 3.85 us  [finish(): pl.pallas_call(finish_kernel, out_shape=(jax.ShapeDtypeStruct((matches, d...]
where the time goes in v4:
time: 66.2 us; the launch traced here: 66 us
  Pallas kernels  60.4 us (91%)
  local copies, waits for them, and re-layouts  3.98 us (6%)
  other arithmetic  0.94 us (1%)
  between operations  0.68 us (1%)
    pallas_call x1, Pallas kernels, exchange(): pl.pallas_call(lambda *refs: exchange_kernel(groups, strips, *refs), out_...  56.5 us
    pallas_call x1, Pallas kernels, finish(): pl.pallas_call(finish_kernel, out_shape=(jax.ShapeDtypeStruct((matches, d...  3.85 us
    reshape x2, local copies, waits for them, and re-layouts, arrange(): images.transpose(0, 1, 4, 3, 2, 5)  3.79 us

profile of v4, /device:TPU:0, one launch (start us, length us, event | category | flops | bytes accessed | tf_op | source)
XLA Modules:
  0.0 66.0 jit_solution(15099614061441310077)
XLA Ops:
  0.6 0.1 pad.1.clone
  0.7 0.7 %convert_multiply_fusion = f32[2,2]{1,0:T(2,128)S(1)} fusion(s32[2,2]{1,0:T(2,128)} %param.5), kind=kLoop, calls=%fused_computation.10 | loop fusion | flops 8 | bytes 32 | tf_op jit(solution)/shard_map/mul | solution.py:28
  1.4 0.1 iota_add_fusion
  1.4 0.1 multiply_convert_fusion.1
  1.6 0.1 fusion.9
  1.7 0.1 pad_maximum_fusion
  1.8 3.2 %reshape.83 = bf16[2,16,8,16,256]{4,2,3,1,0:T(8,128)(2,1)S(1)} reshape(bf16[2,16,8,16,2,128]{5,4,2,3,1,0:T(2,128)(2,1)} %bitcast.7) | data formatting | bytes 4194304 | tf_op jit(solution)/shard_map/reshape | solution.py:418
  4.9 0.0 copy-start
  4.9 0.6 copy.9.refs_2_
  5.6 0.0 copy-done
  5.6 56.5 %exchange.1 = (f32[2,16,2,4,2,16,128]{6,5,4,3,2,1,0:T(8,128)S(1)}, bf16[2,10,2,4,2,16,128]{6,5,4,3,2,1,0:T(8,128)(2,1)S(1)}, bf16[2,10,2,4,2,16,128]{6,5,4,3,2,1...) custom-call(s32[2,2]{1,0:T(2,128)S(1)} %copy-done, f32[4,2,128]{2,1,0:T(2,128)S(1)} %bitcast.6, ...), custom_call_target="tpu_custom_call" | custom-call | tf_op jit(solution)/shard_map/exchange/pallas_call | solution.py:307
  62.1 3.8 %finish.1 = (bf16[2,2,2,16,4096]{4,3,2,1,0:T(8,128)(2,1)}, bf16[2,2,16,4096]{3,2,1,0:T(8,128)(2,1)}) custom-call(s32[2,2]{1,0:T(2,128)S(1)} %copy-done, f32[2,16,2,4,2,16,128]{6,5,4,3,2,1,0:T(8,128)S(1)} %get-tuple-element.6.looks_ref, bf16[2,10,2,4,2,16,128]{6,5,4,3,2,1,0:T(8,128)(2,1)S(1)} %get-tuple-element.7.low_ref, ...), custom_call_target="tpu_custom_call" | custom-call | tf_op jit(solution)/shard_map/finish/pallas_call | solution.py:391
  (4 shorter events, 0.0 us)
Async XLA Ops:
  4.9 0.7 %copy-start = (s32[2,2]{1,0:T(2,128)S(1)}, s32[2,2]{1,0:T(2,128)}, u32[]{:S(2)}) copy-start(s32[2,2]{1,0:T(2,128)} %places_ref.1) | copy-start | bytes 52
